TPU v7x, 256 devices: a whole 4x4x8 slice. The times are simulated.
256 devices in a mesh: dp: 4 (over y), pipe: 2 (over core), gz: 8 (over z), gy: 4 (over x).
Axes of the slice: x: 4, y: 4, z: 8, core: 2. Of those that a mesh axis runs over, the one named last changes fastest.
Arguments:
- volumes: bfloat16 [8, 32, 16, 32, 128], P('dp', None, 'gz', 'gy'), may hold values from -6 to 6
- conv_one: bfloat16 [32, 4, 3, 3, 3], replicated, may hold values from -0.625 to 0.625
- conv_two: bfloat16 [64, 32, 3, 3, 3], replicated, may hold values from -0.21875 to 0.21875
- cotangent: bfloat16 [8, 64, 8, 16, 64], P('dp', None, 'gz', 'gy'), may hold values from -24 to 24
Outputs:
- boundary_acts: bfloat16 [8, 32, 16, 32, 128], P('dp', None, 'gz', 'gy')
- boundary_grads: bfloat16 [8, 32, 16, 32, 128], P('dp', None, 'gz', 'gy')
- grad_conv_one: float32 [32, 4, 3, 3, 3], replicated
- grad_conv_two: float32 [64, 32, 3, 3, 3], replicated
All inputs are finite; a program needn't handle non-finite values.
Results may differ from a plain program's by a relative error of at most 0.0085.
Values may be sent and summed in bfloat16 or wider, within the bound.
A program may use at most 128 MiB of HBM per device.

v0:
```python
import math

import jax
import jax.numpy as jnp
from jax import lax
from jax.sharding import PartitionSpec as P

LEAK_SLOPE = 0.3
LOG_TWO = math.log(2.0)
LAYOUT = ("NCDHW", "OIDHW", "NCDHW")


def padded_2(cells, sides, width):
    for axis, dim in sides:
        count = lax.axis_size(axis)
        ends = count - 1
        head = lax.slice_in_dim(cells, 0, width, axis=dim)
        tail = lax.slice_in_dim(cells, cells.shape[dim] - width, cells.shape[dim], axis=dim)
        cells = jnp.concatenate(
            [
                lax.ppermute(tail, axis, [(i, (i + 1) % count) for i in range(ends)]),
                cells,
                lax.ppermute(head, axis, [((i + 1) % count, i) for i in range(ends)]),
            ],
            axis=dim,
        )
    return cells


def for_sending(value):
    return jax.tree.map(lambda a: a.astype(jnp.bfloat16) if a.dtype == jnp.float32 else a, value)


def activate(pre_act):
    return LEAK_SLOPE * pre_act + (1.0 - LEAK_SLOPE) * (jax.nn.softplus(pre_act) - LOG_TWO)


def derivative(pre_act):
    return LEAK_SLOPE + (1.0 - LEAK_SLOPE) * jax.nn.sigmoid(pre_act)


def unfold(coarse):
    span_z, span_y, span_x = coarse.shape[1:]
    pieces = coarse.reshape(2, 2, 2, -1, span_z, span_y, span_x)
    ordered = pieces.transpose(3, 4, 0, 5, 1, 6, 2)
    return ordered.reshape(-1, 2 * span_z, 2 * span_y, 2 * span_x)


def average_blocks(grid_in):
    chan_count, span_z, span_y, span_x = grid_in.shape
    grouped = grid_in.reshape(chan_count, span_z // 2, 2, span_y // 2, 2, span_x // 2, 2)
    return jnp.mean(grouped, axis=(2, 4, 6))


def spread_blocks(grid_in):
    chan_count, span_z, span_y, span_x = grid_in.shape
    copied = jnp.broadcast_to(
        grid_in[:, :, None, :, None, :, None], (chan_count, span_z, 2, span_y, 2, span_x, 2)
    )
    return copied.reshape(chan_count, 2 * span_z, 2 * span_y, 2 * span_x) / 8.0


def pad_width(grid_in):
    return jnp.pad(grid_in, ((0, 0), (0, 0), (0, 0), (1, 1)))


def convolve_valid(grid_in, kernel):
    result = lax.conv_general_dilated(
        pad_width(grid_in)[None],
        kernel,
        (1, 1, 1),
        "VALID",
        dimension_numbers=LAYOUT,
        preferred_element_type=jnp.float32,
    )
    return result[0]


def kernel_grad(padded, grad_out):
    out_count = grad_out.shape[0]
    in_count = padded.shape[0]
    span_z, span_y, span_x = grad_out.shape[1:]
    flat_out = grad_out.reshape(out_count, -1)
    products = []
    for off_z in range(3):
        for off_y in range(3):
            for off_x in range(3):
                shifted = padded[
                    :, off_z : off_z + span_z, off_y : off_y + span_y, off_x : off_x + span_x
                ].reshape(in_count, -1)
                products.append(
                    jnp.einsum("op,cp->oc", flat_out, shifted, preferred_element_type=jnp.float32)
                )
    return jnp.stack(products, axis=-1).reshape(out_count, in_count, 3, 3, 3)


def extend(grid_in):
    return padded_2(grid_in, (("gz", 1), ("gy", 2)), 1)


def head_margin(extended):
    return unfold(extended)[:, 1:-1, 1:-1, :]


def first_forward(extended, kernel):
    pre_act = convolve_valid(head_margin(extended), kernel)
    return average_blocks(activate(pre_act)).astype(jnp.bfloat16)


def first_backward(extended, back_in, kernel):
    fine_grid = head_margin(extended)
    pre_act = convolve_valid(fine_grid, kernel)
    first_grad = (derivative(pre_act) * spread_blocks(back_in.astype(jnp.float32))).astype(
        jnp.bfloat16
    )
    return kernel_grad(pad_width(fine_grid), first_grad)


def second_slope(extended, cot_part, kernel):
    pre_act = convolve_valid(extended, kernel)
    return (derivative(pre_act) * spread_blocks(cot_part.astype(jnp.float32))).astype(jnp.bfloat16)


def per_device(volumes, conv_one, conv_two, cotangent):
    micro_count = volumes.shape[0]
    flipped = jnp.flip(conv_two, axis=(2, 3, 4)).transpose(1, 0, 2, 3, 4)
    empty_one = jnp.zeros(conv_one.shape, jnp.float32)
    empty_two = jnp.zeros(conv_two.shape, jnp.float32)
    batch_count = micro_count * lax.axis_size("dp")
    half_count = micro_count // 2
    offset = lax.axis_index("pipe") * half_count
    own_volumes = lax.dynamic_slice_in_dim(volumes, offset, half_count, 0)
    own_cotangent = lax.dynamic_slice_in_dim(cotangent, offset, half_count, 0)
    grad_one = empty_one
    grad_two = empty_two
    extended = extend(own_volumes[0])
    pooled = first_forward(extended, conv_one)
    pooled_ext = extend(pooled)
    second_grad = second_slope(pooled_ext, own_cotangent[0], conv_two)
    grad_ext = extend(second_grad)
    grad_two = grad_two + kernel_grad(pad_width(pooled_ext), second_grad)
    back_out = convolve_valid(grad_ext, flipped).astype(jnp.bfloat16)
    grad_one = grad_one + first_backward(extended, back_out, conv_one)
    pooled_list = [pooled]
    back_list = [back_out]
    all_pooled, all_back = (
        lax.all_gather(jnp.stack(pooled_list), "pipe", axis=0, tiled=True),
        lax.all_gather(for_sending(jnp.stack(back_list)), "pipe", axis=0, tiled=True),
    )
    total_one, total_two = lax.psum((grad_one, grad_two), ("dp", "pipe", "gz", "gy"))
    return (all_pooled, all_back, total_one / batch_count, total_two / batch_count)


def solution(mesh):
    in_specs = (P("dp", None, "gz", "gy", None), P(), P(), P("dp", None, "gz", "gy", None))
    out_specs = (P("dp", None, "gz", "gy", None), P("dp", None, "gz", "gy", None), P(), P())
    return jax.shard_map(
        per_device, mesh=mesh, in_specs=in_specs, out_specs=out_specs, check_vma=False
    )
```

profile of v0, /device:TPU:1, one launch (start us, length us, event | category | flops | bytes accessed | tf_op | source)
XLA Modules:
  0.0 615.6 jit_solution(1726338462379814897)
XLA Ops:
  8.2 4.4 collective-permute-start
  26.5 15.9 %copy.254 = bf16[4,4,2,10,2,128,2]{0,6,5,4,3,2,1:T(2,128)(2,1)} copy(bf16[4,4,2,10,2,128,2]{5,0,6,4,2,3,1:T(4,128)(2,1)S(1)} %bitcast.565) | data formatting | bytes 655360 | tf_op jit(solution)/shard_map/transpose | solution.py:45
  42.4 6.8 %slice.314 = bf16[4,6,18,256]{0,3,2,1:T(8,128)(2,1)} slice(bf16[4,8,20,256]{0,3,2,1:T(8,128)(2,1)} %bitcast.545), slice={[0:4], [1:7], [1:19], [0:256]} | slice | bytes 442368 | tf_op jit(solution)/shard_map/slice | solution.py:102
  49.2 5.7 copy.372
  56.1 4.7 copy.257
  61.9 23.6 %fusion.25 = f32[4,16,8,33,32]{4,2,3,1,0:T(8,128)} fusion(bf16[32,4,3,3,3]{0,1,4,3,2:T(4,128)(2,1)S(1)} %copy-done.6, bf16[4,6,18,1,7,2]{4,0,5,2,1,3:T(4,128)(2,1)S(1)} %slice.315, bf16[4,6,18,1,8,33]{4,0,5,2,1,3:T(4,128)(2,1)} %copy.257), kind=kOutput, calls=%fused_computation.31 | convolution fusion | flops 117510912 | bytes 2409792 | tf_op jit(solution)/shard_map/conv_general_dilated | solution.py:68
  85.5 10.7 %copy.258 = f32[4,16,8,33,32]{3,4,2,1,0:T(8,128)} copy(f32[4,16,8,33,32]{4,2,3,1,0:T(8,128)} %fusion.25) | data formatting | bytes 4325376 | tf_op jit(solution)/shard_map/conv_general_dilated | solution.py:68
  96.3 6.9 %add_divide_fusion = (f32[4,16,8,33,32]{3,4,2,1,0:T(8,128)}, f32[4,16,8,33,32]{3,4,2,1,0:T(8,128)S(1)}) fusion(f32[4,16,8,33,32]{3,4,2,1,0:T(8,128)} %copy.258, pred[8,33]{1,0:T(8,128)(4,1)S(1)} %copy-done.4), kind=kLoop, calls=%fused_computation.4 | loop fusion | flops 2162688 | bytes 6488328 | tf_op jit(solution)/shard_map/div | solution.py:39
  103.2 11.5 %copy.259 = f32[4,16,8,33,32]{3,2,4,1,0:T(8,128)} copy(f32[4,16,8,33,32]{3,4,2,1,0:T(8,128)S(1)} %get-tuple-element.29) | data formatting | bytes 4325376 | tf_op jit(solution)/shard_map/conv_general_dilated | solution.py:68
  114.7 7.4 %reshape.145 = f32[4,16,1,264,32]{3,4,1,0,2:T(8,128)} reshape(f32[4,16,8,33,32]{3,2,4,1,0:T(8,128)} %copy.259) | data formatting | bytes 4325376 | tf_op jit(solution)/shard_map/conv_general_dilated | solution.py:68
  123.8 4.7 copy.260
  128.5 28.5 %fusion.3 = f32[32,2,8,128]{0,3,2,1:T(8,128)S(1)} fusion(f32[32,2,2,8,2,128,2]{0,6,5,4,3,2,1:T(2,128)} %bitcast.557), kind=kLoop, calls=%fused_computation.5 | loop fusion | flops 5701632 | bytes 2359296 | tf_op jit(solution)/shard_map/reduce_sum | solution.py:52
  162.7 4.6 collective-permute-done.5
  171.8 6.3 %all-gather = bf16[64,2,8,128]{3,0,2,1:T(8,128)(2,1)S(1)} all-gather(bf16[32,2,8,128]{3,0,2,1:T(8,128)(2,1)S(1)} %multiply_convert_fusion), channel_id=2, replica_groups=mesh['dp'=4,'pipe'=2,'gz'=8,'gy'=4] {'pipe'}, dimensions={0}, use_global_device_ids=true | all-gather | bytes 393216 | tf_op jit(solution)/shard_map/all_gather | solution.py:147
  178.1 14.9 %copy.277 = f32[4,16,8,33,32]{3,2,4,1,0:T(8,128)} copy(f32[4,16,8,33,32]{3,4,2,1,0:T(8,128)} %get-tuple-element.28) | data formatting | bytes 4325376 | tf_op jit(solution)/shard_map/div | solution.py:39
  192.9 7.6 %reshape.147 = f32[4,16,1,264,32]{3,4,1,0,2:T(8,128)} reshape(f32[4,16,8,33,32]{3,2,4,1,0:T(8,128)} %copy.277) | data formatting | bytes 4325376 | tf_op jit(solution)/shard_map/div | solution.py:39
  213.9 4.9 collective-permute-start.8
  221.2 4.4 collective-permute-done.9
  225.9 4.3 collective-permute-start.10
  231.5 244.8 %all-reduce.5.cloned.1.call-done = f32[64,32,3,3,3]{0,1,4,3,2:T(8,128)} async-done(((f32[64,32,3,3,3]{0,1,4,3,2:T(8,128)}), f32[64,32,3,3,3]{0,1,4,3,2:T(8,128)}) %all-reduce.5.cloned.1.call-update) | async-done | bytes 221200 | tf_op jit(solution)/shard_map/psum | solution.py:150
  482.6 4.3 convert_multiply_fusion
  487.4 7.3 %broadcast_in_dim.29 = f32[32,2,2,8,2,128,2]{0,6,5,4,3,2,1:T(2,128)} broadcast(f32[32,2,8,128]{0,3,2,1:T(8,128)S(1)} %copy.279), dimensions={0,1,3,5} | broadcast | bytes 2359296 | tf_op jit(solution)/shard_map/broadcast_in_dim | solution.py:57
  494.7 5.4 copy.280
  526.9 76.9 %psum.14 = f32[32,4,3,3,3]{0,1,4,3,2:T(4,128)S(1)} all-reduce(f32[32,4,3,3,3]{0,1,4,3,2:T(4,128)S(1)} %bitcast.568), channel_id=1, replica_groups=mesh['dp'=4,'pipe'=2,'gz'=8,'gy'=4] {'dp','pipe','gz','gy'}, use_global_device_ids=true, to_apply=%region_1.2 | all-reduce | flops 3456 | bytes 27648 | tf_op jit(solution)/shard_map/psum | solution.py:150
  (151 shorter events, 84.1 us)
Async XLA Ops:
  7.2 1.0 copy-start
  7.2 469.1 %all-reduce.5.cloned.1.call-start = ((), (), s32[]{:S(2)}) async-start(), calls=%async_computation | async-start | bytes 884736 | tf_op jit(solution)/shard_map/psum | solution.py:150
  8.2 5.7 collective-permute-start
  12.5 5.2 collective-permute-start.1
  17.8 4.4 collective-permute-start.2
  20.9 5.0 collective-permute-start.3
  55.4 6.6 %copy-start.6 = (bf16[32,4,3,3,3]{0,1,4,3,2:T(4,128)(2,1)S(1)}, bf16[32,4,3,3,3]{0,1,4,3,2:T(4,128)(2,1)}, u32[]{:S(2)}) copy-start(bf16[32,4,3,3,3]{0,1,4,3,2:T(4,128)(2,1)} %param.5) | copy-start | bytes 20740
  85.5 10.7 %copy-start.4 = (pred[8,33]{1,0:T(8,128)(4,1)S(1)}, pred[8,33]{1,0:T(8,128)(4,1)}, u32[]{:S(2)}) copy-start(pred[8,33]{1,0:T(8,128)(4,1)} %constant.59) | copy-start | bytes 796
  128.5 33.7 %copy-start.3 = (bf16[2,64,1,4,64]{4,3,2,1,0:T(4,128)(2,1)S(1)}, bf16[2,64,1,4,64]{4,3,2,1,0:T(4,128)(2,1)}, u32[]{:S(2)}) copy-start(bf16[2,64,1,4,64]{4,3,2,1,0:T(4,128)(2,1)} %param.7) | copy-start | bytes 196612
  157.4 5.4 collective-permute-start.4
  160.9 6.4 %collective-permute-start.5 = (bf16[32,1,8,128]{3,0,2,1:T(8,128)(2,1)S(1)}, bf16[32,1,8,128]{3,0,2,1:T(8,128)(2,1)S(1)}, u32[]{:S(2)}, u32[]{:S(2)}) collective-permute-start(bf16[32,1,8,128]{3,0,2,1:T(8,128)(2,1)S(1)} %get-tuple-element.41), channel_id=1, source_target_pairs={{4,0},{8,4},{12,8},{16,12},{20,16},{24,20},{28,24},{5,1},{9,5},{13... | collective-permute-start | bytes 196616 | tf_op jit(solution)/shard_map/ppermute | solution.py:23
  167.3 34.0 %collective-permute-start.6 = (bf16[32,4,1,128]{3,0,2,1:T(8,128)(2,1)S(1)}, bf16[32,4,1,128]{3,0,2,1:T(8,128)(2,1)S(1)}, u32[]{:S(2)}, u32[]{:S(2)}) collective-permute-start(bf16[32,4,1,128]{3,0,2,1:T(8,128)(2,1)S(1)} %get-tuple-element.36), channel_id=1, source_target_pairs={{0,1},{1,2},{2,3},{4,5},{5,6},{6,7},{8,9},{9,10},{10,11},{12,13},{... | collective-permute-start | bytes 98312 | tf_op jit(solution)/shard_map/ppermute | solution.py:21
  170.5 30.9 %collective-permute-start.7 = (bf16[32,4,1,128]{3,0,2,1:T(8,128)(2,1)S(1)}, bf16[32,4,1,128]{3,0,2,1:T(8,128)(2,1)S(1)}, u32[]{:S(2)}, u32[]{:S(2)}) collective-permute-start(bf16[32,4,1,128]{3,0,2,1:T(8,128)(2,1)S(1)} %get-tuple-element.37), channel_id=1, source_target_pairs={{1,0},{2,1},{3,2},{5,4},{6,5},{7,6},{9,8},{10,9},{11,10},{13,12},{... | collective-permute-start | bytes 98312 | tf_op jit(solution)/shard_map/ppermute | solution.py:23
  203.9 1.0 copy-start.5
  203.9 1.0 copy-start.7
  213.9 7.3 %collective-permute-start.8 = (bf16[64,1,8,128]{3,2,1,0:T(8,128)(2,1)S(1)}, bf16[64,1,8,128]{3,2,1,0:T(8,128)(2,1)S(1)}, u32[]{:S(2)}, u32[]{:S(2)}) collective-permute-start(bf16[64,1,8,128]{3,2,1,0:T(8,128)(2,1)S(1)} %get-tuple-element.34), channel_id=1, source_target_pairs={{0,4},{4,8},{8,12},{12,16},{16,20},{20,24},{24,28},{1,5},{5,9},{9,... | collective-permute-start | bytes 393224 | tf_op jit(solution)/shard_map/ppermute | solution.py:21
  218.7 6.9 %collective-permute-start.9 = (bf16[64,1,8,128]{3,2,1,0:T(8,128)(2,1)S(1)}, bf16[64,1,8,128]{3,2,1,0:T(8,128)(2,1)S(1)}, u32[]{:S(2)}, u32[]{:S(2)}) collective-permute-start(bf16[64,1,8,128]{3,2,1,0:T(8,128)(2,1)S(1)} %get-tuple-element.35), channel_id=1, source_target_pairs={{4,0},{8,4},{12,8},{16,12},{20,16},{24,20},{28,24},{5,1},{9,5},{13... | collective-permute-start | bytes 393224 | tf_op jit(solution)/shard_map/ppermute | solution.py:23
  220.3 0.8 copy-start.2
  225.9 252.4 %collective-permute-start.10 = (bf16[64,4,1,128]{3,2,1,0:T(2,128)(2,1)S(1)}, bf16[64,4,1,128]{3,2,1,0:T(2,128)(2,1)S(1)}, u32[]{:S(2)}, u32[]{:S(2)}) collective-permute-start(bf16[64,4,1,128]{3,2,1,0:T(2,128)(2,1)S(1)} %get-tuple-element.30), channel_id=1, source_target_pairs={{0,1},{1,2},{2,3},{4,5},{5,6},{6,7},{8,9},{9,10},{10,11},{12,13},{... | collective-permute-start | bytes 196616 | tf_op jit(solution)/shard_map/ppermute | solution.py:21
  230.2 248.1 %collective-permute-start.11 = (bf16[64,4,1,128]{3,2,1,0:T(2,128)(2,1)S(1)}, bf16[64,4,1,128]{3,2,1,0:T(2,128)(2,1)S(1)}, u32[]{:S(2)}, u32[]{:S(2)}) collective-permute-start(bf16[64,4,1,128]{3,2,1,0:T(2,128)(2,1)S(1)} %get-tuple-element.31), channel_id=1, source_target_pairs={{1,0},{2,1},{3,2},{5,4},{6,5},{7,6},{9,8},{10,9},{11,10},{13,12},{... | collective-permute-start | bytes 196616 | tf_op jit(solution)/shard_map/ppermute | solution.py:23
  500.1 11.8 %slice-start = ((s8[10485760]{0:T(1024)(128)(4,1)}), s8[4194304]{0:T(1024)(128)(4,1)S(1)}, s32[]{:S(2)}) async-start(s8[10485760]{0:T(1024)(128)(4,1)} %bitcast.548), calls=%async_computation.1 | async-start | bytes 8388608
  502.9 9.1 %slice-start.1 = ((s8[10485760]{0:T(1024)(128)(4,1)}), s8[4194304]{0:T(1024)(128)(4,1)S(1)}, s32[]{:S(2)}) async-start(s8[10485760]{0:T(1024)(128)(4,1)} %bitcast.548), calls=%async_computation.2 | async-start | bytes 8388608
  507.4 4.5 slice-start.2
  524.9 83.4 %copy-start.1 = (bf16[2,32,2,8,128]{4,3,2,1,0:T(8,128)(2,1)S(1)}, bf16[2,32,2,8,128]{4,3,2,1,0:T(8,128)(2,1)}, u32[]{:S(2)}) copy-start(bf16[2,32,2,8,128]{4,3,2,1,0:T(8,128)(2,1)} %param.4) | copy-start | bytes 786436
Sparse Core Ops, SparseCore 0:
  221.2 255.0 all-reduce.4
where the time goes:
time: 625 us; the launch traced here: 616 us
  waiting for transfers between devices  262 us (42%)
  local copies, waits for them, and re-layouts  120 us (19%)
  blocking collectives  85.8 us (14%)
  matrix products  60.2 us (10%)
  other arithmetic  42.4 us (7%)
  starting transfers between devices  31.1 us (5%)
  between operations  15.1 us (2%)
    psum x1, waiting for transfers between devices, per_device(): lax.psum((grad_one, grad_two), ('dp', 'pipe', 'gz', 'gy'))  245 us
    psum x1, blocking collectives, per_device(): lax.psum((grad_one, grad_two), ('dp', 'pipe', 'gz', 'gy'))  76.9 us
    conv_general_dilated x12, local copies, waits for them, and re-layouts, convolve_valid(): lax.conv_general_dilated(pad_width(grid_in)[None], kernel, (1, 1, 1), 'VA...  43.1 us
    dot_general x54, matrix products, kernel_grad(): jnp.einsum('op,cp->oc', flat_out, shifted, preferred_element_type=jnp.flo...  30.5 us
    conv_general_dilated x3, matrix products, convolve_valid(): lax.conv_general_dilated(pad_width(grid_in)[None], kernel, (1, 1, 1), 'VA...  29.7 us
    reduce_sum x1, other arithmetic, average_blocks(): return jnp.mean(grouped, axis=(2, 4, 6))  28.5 us
    ppermute x6, starting transfers between devices, padded_2(): lax.ppermute(tail, axis, [(i, (i + 1) % count) for i in range(ends)])  23.3 us
    div x4, local copies, waits for them, and re-layouts, derivative(): return LEAK_SLOPE + (1.0 - LEAK_SLOPE) * jax.nn.sigmoid(pre_act)  22.7 us
  transfers between devices with their start and end apart: 13, of which 6 were waited for; matrix products, arithmetic and copies ran while one was open for 4% of the time, Pallas kernels for 0%

commit v1 on v0

v1 whole, which is shorter than its diff:
```python
import functools
import math

import jax
import jax.numpy as jnp
from jax import lax
from jax.experimental import pallas as pl
from jax.experimental.pallas import tpu as pltpu
from jax.sharding import PartitionSpec as P

LEAK = 0.3
REST = 1.0 - LEAK
LOG_TWO = math.log(2.0)
MESH = pl.DeviceIdType.MESH
F32 = jnp.float32
BF16 = jnp.bfloat16
LANES = 128
DIRS = tuple((dz, dy) for dz in (-1, 0, 1) for dy in (-1, 0, 1) if (dz, dy) != (0, 0))


def mm(a, b):
    return lax.dot_general(a, b, (((1,), (0,)), ((), ())), preferred_element_type=F32)


def mm_nt(a, b):
    return lax.dot_general(a, b, (((1,), (1,)), ((), ())), preferred_element_type=F32)


def eye(n, m):
    return (
        lax.broadcasted_iota(jnp.int32, (n, m), 0) == lax.broadcasted_iota(jnp.int32, (n, m), 1)
    ).astype(BF16)


def to_right(v):
    lane = lax.broadcasted_iota(jnp.int32, v.shape, 1)
    return jnp.where(lane == 0, 0.0, pltpu.roll(v, 1, axis=1))


def to_left(v):
    lane = lax.broadcasted_iota(jnp.int32, v.shape, 1)
    return jnp.where(lane == LANES - 1, 0.0, pltpu.roll(v, LANES - 1, axis=1))


def slope_of(v):
    return LEAK + REST / (1.0 + jnp.exp(-v))


def act_and_slope(v):
    e = jnp.exp(-jnp.abs(v))
    r = 1.0 / (1.0 + e)
    act = LEAK * v + REST * (jnp.maximum(v, 0.0) + jnp.log(1.0 + e) - LOG_TWO)
    return act, LEAK + REST * jnp.where(v >= 0.0, r, e * r)


def part(d, n):
    if d == 0:
        return pl.ds(1, n), pl.ds(1, n)
    if d == 1:
        return pl.ds(n, 1), pl.ds(0, 1)
    return pl.ds(1, 1), pl.ds(n + 1, 1)


def step_kernel(
    dims,
    vol, one_ref, two_ref, cot_ref,
    acts_out, grads_out, one_out, two_out,
    raw, rawf, fine, pool, grad2, slope1, shifted, cots, sel, w1, w2, wb,
    sum1, sum2, flat1, flat2, half1, half2,
    ga, ra, sb, rb, sc, rc, fd,
    qa, qra, qs, qrb, qsc, qrc, qf,
    local_sem, out_ssem, out_rsem,
    h_ssem, h_rsem,
    pair_ssem, pair_rsem, line_ssem, line_rsem, plane_ssem, plane_rsem,
):
    nd, nz, ny, sz, sy, batch = dims
    rows = sz * sy
    core = lax.axis_index("pipe")
    iz, iy, idp = lax.axis_index("gz"), lax.axis_index("gy"), lax.axis_index("dp")
    other = 1 - core
    plane = nd * ny
    me_plane = idp * ny + iy

    def on_line(off):
        return lax.rem(iz + off, nz)

    def on_plane(off):
        q = lax.rem(me_plane + off, plane)
        return q, {"dp": q // ny, "gy": lax.rem(q, ny)}

    def exists(dz, dy):
        ok = jnp.bool_(True)
        if dz == 1:
            ok = jnp.logical_and(ok, iz < nz - 1)
        if dz == -1:
            ok = jnp.logical_and(ok, iz > 0)
        if dy == 1:
            ok = jnp.logical_and(ok, iy < ny - 1)
        if dy == -1:
            ok = jnp.logical_and(ok, iy > 0)
        return ok

    def neighbour(dz, dy):
        return {"gz": lax.rem(iz + dz + nz, nz), "gy": lax.rem(iy + dy + ny, ny)}

    def halo_copy(k, ref, d):
        dz, dy = DIRS[d]
        (fz, tz), (fy, ty) = part(dz, ref.shape[0] - 2), part(dy, ref.shape[1] - 2)
        return pltpu.make_async_remote_copy(
            src_ref=ref.at[fz, fy],
            dst_ref=ref.at[tz, ty],
            send_sem=h_ssem.at[k, d],
            recv_sem=h_rsem.at[k, d],
            device_id=neighbour(dz, dy),
            device_id_type=MESH,
        )

    def halo_clear(ref):
        for dz, dy in DIRS:
            _, tz = part(dz, ref.shape[0] - 2)
            _, ty = part(dy, ref.shape[1] - 2)

            @pl.when(jnp.logical_not(exists(-dz, -dy)))
            def _():
                view = ref.at[tz, ty]
                view[...] = jnp.zeros(view.shape, view.dtype)

    def halo_send(k, ref):
        for d, (dz, dy) in enumerate(DIRS):

            @pl.when(exists(dz, dy))
            def _():
                halo_copy(k, ref, d).start()

    def halo_arrive(k, ref):
        for d, (dz, dy) in enumerate(DIRS):

            @pl.when(exists(-dz, -dy))
            def _():
                halo_copy(k, ref, d).wait_recv()

    def halo_sent(k, ref):
        for d, (dz, dy) in enumerate(DIRS):

            @pl.when(exists(dz, dy))
            def _():
                halo_copy(k, ref, d).wait_send()

    def to_pair(k, src, dst):
        return pltpu.make_async_remote_copy(
            src_ref=src, dst_ref=dst, send_sem=pair_ssem.at[k], recv_sem=pair_rsem.at[k],
            device_id={"pipe": other}, device_id_type=MESH,
        )

    def to_line(k, off, src, dst):
        return pltpu.make_async_remote_copy(
            src_ref=src, dst_ref=dst, send_sem=line_ssem.at[k, off - 1], recv_sem=line_rsem.at[k, off - 1],
            device_id={"gz": on_line(off)}, device_id_type=MESH,
        )

    def to_plane(k, off, src, dst):
        return pltpu.make_async_remote_copy(
            src_ref=src, dst_ref=dst, send_sem=plane_ssem.at[k, off - 1], recv_sem=plane_rsem.at[k, off - 1],
            device_id=on_plane(off)[1], device_id_type=MESH,
        )

    fetch = pltpu.make_async_copy(vol.at[core], raw, local_sem.at[0])
    fetch.start()
    barrier = pltpu.get_barrier_semaphore()
    pl.semaphore_signal(barrier, inc=1, device_id={"pipe": other}, device_id_type=MESH)
    count = jnp.int32(1 + (nz - 1) + (plane - 1))
    for dz, dy in DIRS:
        if dz != 0 and dy != 0:

            @pl.when(exists(dz, dy))
            def _():
                pl.semaphore_signal(barrier, inc=1, device_id=neighbour(dz, dy), device_id_type=MESH)

            count = count + exists(dz, dy).astype(jnp.int32)
    for off in range(1, plane):
        pl.semaphore_signal(barrier, inc=1, device_id=on_plane(off)[1], device_id_type=MESH)
    for off in range(1, nz):
        pl.semaphore_signal(barrier, inc=1, device_id={"gz": on_line(off)}, device_id_type=MESH)

    halo_clear(fine)
    halo_clear(pool)
    halo_clear(grad2)

    fetch.wait()
    rawf[...] = raw[...].astype(F32)

    def spread_row(z, y):
        t = rawf[pl.ds(z * sy + y, 32, stride=rows), :]
        sub = lax.broadcasted_iota(jnp.int32, t.shape, 0)
        odd = (sub & 4) != 0
        low = jnp.where(odd, to_right(t), t)
        high = jnp.where(odd, t, to_left(t))
        for a in range(2):
            for b in range(2):
                j = 8 * (2 * a + b)
                both = jnp.concatenate([low[j : j + 8], high[j : j + 8]], axis=0)
                fine[2 * z + a + 1, 2 * y + b + 1] = both.astype(BF16)

    def loop_rows(body):
        def outer(z, _):
            def inner(y, __):
                body(z, y)
                return 0

            lax.fori_loop(0, sy, inner, 0)
            return 0

        lax.fori_loop(0, sz, outer, 0)

    def loop_pairs(z, body):
        def inner(p, _):
            body(z, p)
            return 0

        lax.fori_loop(0, sy // 2, inner, 0)

    loop_rows(spread_row)
    pl.semaphore_wait(barrier, count)
    halo_send(0, fine)

    row = lax.broadcasted_iota(jnp.int32, (128, 256), 0)
    lane = lax.broadcasted_iota(jnp.int32, (128, 256), 1)
    tap = row >> 2
    by3 = (tap * 11) >> 5
    by9 = (by3 * 11) >> 5
    tx, ty, tz = tap - 3 * by3, by3 - 3 * by9, by9
    for d in range(27):
        qa[0, 4 * d : 4 * d + 4, 0:32] = one_ref[d].astype(F32)
    qa[0, 108:128, 0:32] = jnp.zeros((20, 32), F32)
    one_t = mm_nt(eye(32, 32), qa[0, :, 0:32].astype(BF16)).astype(BF16)
    for s in range(8):
        a, b, c = s >> 2, (s >> 1) & 1, s & 1
        fx = tx + c
        slot = fx + 1 - 2 * (fx & 1)
        target = (tz + a) * 64 + (ty + b) * 16 + slot * 4 + (row & 3)
        hit = jnp.logical_and(lane == target, row < 108)
        sel[s] = jnp.where(hit, 1.0, 0.0).astype(BF16)
        w1[32 * s : 32 * s + 32, :] = mm(one_t, sel[s]).astype(BF16)
    for dx in range(3):
        taps = jnp.concatenate([two_ref[3 * j + dx] for j in range(9)], axis=0)
        w2[64 * dx : 64 * dx + 64, :] = mm_nt(eye(64, 64), taps).astype(BF16)
    for ex in range(3):
        blocks = [two_ref[3 * (8 - j) + 2 - ex].astype(F32) for j in range(9)]
        for j in range(0, 8, 2):
            pair = jnp.concatenate([blocks[j], blocks[j + 1]], axis=1)
            wb[32 * ex : 32 * ex + 32, 64 * j : 64 * j + 128] = pair.astype(BF16)
        wb[32 * ex : 32 * ex + 32, 512:576] = blocks[8].astype(BF16)
    double = (
        (lax.broadcasted_iota(jnp.int32, (64, LANES), 1) >> 1)
        == lax.broadcasted_iota(jnp.int32, (64, LANES), 0)
    ).astype(BF16)
    for y in range(sy // 2):
        cots[y] = mm(cot_ref[core, y], double) * 0.125

    def windows(z, p):
        return jnp.concatenate(
            [fine[pl.ds(2 * z, 4), pl.ds(4 * p + 2 * j, 4)].reshape(256, LANES) for j in range(2)], axis=1
        )

    def first_pair(z, p):
        pre = mm(w1[...], windows(z, p))
        for j in range(2):
            y = 2 * p + j
            total = jnp.zeros((32, LANES), F32)
            for s in range(8):
                act, slope = act_and_slope(pre[32 * s : 32 * s + 32, LANES * j : LANES * j + LANES])
                total = total + act
                slope1[z, y, 32 * s : 32 * s + 32, :] = slope
            mean = total * 0.125
            pool[z + 1, y + 1] = mean.astype(BF16)
            flat1[pl.ds(z * sy + y, 32, stride=rows), :] = mean

    halo_arrive(0, fine)
    for z in range(sz):
        loop_pairs(z, first_pair)
    halo_send(1, pool)
    half1[...] = flat1[...].astype(BF16)

    def out_copies(k, half, out):
        here = pltpu.make_async_copy(half, out.at[core], local_sem.at[1 + k])
        there = pltpu.make_async_remote_copy(
            src_ref=half, dst_ref=out.at[core], send_sem=out_ssem.at[k], recv_sem=out_rsem.at[k],
            device_id={"pipe": other}, device_id_type=MESH,
        )
        return here, there

    for copy in out_copies(0, half1, acts_out):
        copy.start()

    def second_pair(z, p):
        cells = jnp.concatenate(
            [pool[pl.ds(z, 3), pl.ds(2 * p + j, 3)].reshape(288, LANES) for j in range(2)], axis=1
        )
        prod = mm(w2[...], cells)
        for j in range(2):
            mine = prod[:, LANES * j : LANES * j + LANES]
            pre = to_right(mine[0:64]) + mine[64:128] + to_left(mine[128:192])
            g = (slope_of(pre) * cots[p]).astype(BF16)
            grad2[z + 1, 2 * p + j + 1] = g
            wide = g.astype(F32)
            right = to_right(wide).astype(BF16)
            cols = slice(LANES * j, LANES * j + LANES)
            shifted[z, p, 0:64, cols] = to_left(wide).astype(BF16)
            shifted[z, p, 64:128, cols] = g
            shifted[z, p, 128:192, cols] = right
            shifted[z, p, 192:256, cols] = right

    halo_arrive(1, pool)
    for z in range(sz):
        loop_pairs(z, second_pair)
    halo_send(2, grad2)

    sum2[...] = jnp.zeros(sum2.shape, F32)

    def second_terms(z, p):
        cells = jnp.concatenate(
            [pool[pl.ds(z, 3), pl.ds(2 * p + j, 3)].reshape(288, LANES) for j in range(2)], axis=1
        )
        sum2[...] += mm_nt(cells, shifted[z, p])

    for z in range(sz):
        loop_pairs(z, second_terms)
    for r in range(9):
        ga[r // 8, r % 8] = sum2[32 * r : 32 * r + 32, 0:128]
    keep = lax.broadcasted_iota(jnp.int32, (16, LANES), 1) < 64
    for r in range(9):
        lo, hi = sum2[16 * r : 16 * r + 16, 128:256], sum2[144 + 16 * r : 160 + 16 * r, 128:256]
        at = 288 + 16 * r
        ga[at // 256, at % 256 // 32, at % 32 : at % 32 + 16] = jnp.where(keep, lo, hi)
    ga[1, 5, 16:32] = jnp.zeros((16, LANES), F32)
    ga[1, 6] = jnp.zeros((32, LANES), F32)
    ga[1, 7] = jnp.zeros((32, LANES), F32)
    to_pair(0, ga.at[other], ra).start()

    sum1[...] = jnp.zeros(sum1.shape, F32)

    def back_pair(z, p):
        cells = jnp.concatenate(
            [grad2[pl.ds(z, 3), pl.ds(2 * p + j, 3)].reshape(576, LANES) for j in range(2)], axis=1
        )
        prod = mm(wb[...], cells)
        grads = []
        for j in range(2):
            y = 2 * p + j
            mine = prod[:, LANES * j : LANES * j + LANES]
            back = to_right(mine[0:32]) + mine[32:64] + to_left(mine[64:96])
            back = back.astype(BF16).astype(F32)
            flat2[pl.ds(z * sy + y, 32, stride=rows), :] = back
            eighth = back * 0.125
            grads.append(
                jnp.concatenate(
                    [(slope1[z, y, 32 * s : 32 * s + 32, :] * eighth).astype(BF16) for s in range(8)], axis=0
                )
            )
        sum1[...] += mm_nt(jnp.concatenate(grads, axis=1), windows(z, p))

    line = range(1, nz)
    flat = range(1, plane)

    halo_arrive(2, grad2)
    loop_pairs(0, back_pair)
    to_pair(0, ga.at[other], ra).wait_recv()
    for j in range(8):
        sb[j] = ga[core, j] + ra[j]
    for off in line:
        to_line(0, off, sb.at[on_line(off)], rb.at[off - 1]).start()
    for z in range(1, sz):
        loop_pairs(z, back_pair)

    folded = jnp.zeros((32, LANES), F32)
    for s in range(8):
        mine = sum1[32 * s : 32 * s + 32, :]
        high = mine.astype(BF16)
        low = (mine - high.astype(F32)).astype(BF16)
        folded = folded + mm_nt(high, sel[s]) + mm_nt(low, sel[s])
    qs[...] = folded
    to_pair(1, qs, qra).start()
    half2[...] = flat2[...].astype(BF16)
    for copy in out_copies(1, half2, grads_out):
        copy.start()

    for off in line:
        to_line(0, off, sb.at[on_line(off)], rb.at[off - 1]).wait_recv()
    total = sb[iz]
    for off in line:
        total = total + rb[off - 1]
    sc[...] = total
    rc[me_plane] = total
    for off in flat:
        to_plane(0, off, sc, rc.at[me_plane]).start()

    to_pair(1, qs, qra).wait_recv()
    both = qs[...] + qra[...]
    mine = jnp.where(core == 0, both[0:16], both[16:32])
    qsc[0] = mine
    qrb[iz] = mine
    for off in line:
        to_line(1, off, qsc.at[0], qrb.at[iz]).start()

    for off in flat:
        to_plane(0, off, sc, rc.at[me_plane]).wait_recv()
    total = rc[0]
    for q in range(1, plane):
        total = total + rc[q]
    fd[core, iz] = total * (1.0 / batch)
    for off in line:
        to_line(2, off, fd.at[core, iz], fd.at[core, iz]).start()

    for off in line:
        to_line(1, off, qsc.at[0], qrb.at[iz]).wait_recv()
    total = qrb[0]
    for q in range(1, nz):
        total = total + qrb[q]
    qsc[1] = total
    qrc[me_plane] = total
    for off in flat:
        to_plane(1, off, qsc.at[1], qrc.at[me_plane]).start()

    for off in line:
        to_line(2, off, fd.at[core, iz], fd.at[core, iz]).wait_recv()
    to_pair(2, fd.at[core], fd.at[core]).start()

    for off in flat:
        to_plane(1, off, qsc.at[1], qrc.at[me_plane]).wait_recv()
    total = qrc[0]
    for q in range(1, plane):
        total = total + qrc[q]
    qf[core] = total * (1.0 / batch)
    to_pair(3, qf.at[core], qf.at[core]).start()

    to_pair(2, fd.at[core], fd.at[core]).wait_recv()
    for j in range(9):
        block = fd[j // 8, j % 8]
        two_out[3 * j] = block[:, 0:64]
        two_out[3 * j + 1] = pltpu.roll(block, 64, axis=1)[:, 0:64]
    for r in range(9):
        at = 288 + 16 * r
        block = fd[at // 256, at % 256 // 32, at % 32 : at % 32 + 16]
        for first, values in ((16 * r, block), (144 + 16 * r, pltpu.roll(block, 64, axis=1))):
            two_out[3 * (first // 32) + 2, first % 32 : first % 32 + 16, :] = values[:, 0:64]
    to_pair(3, qf.at[core], qf.at[core]).wait_recv()
    turned = jnp.transpose(jnp.concatenate([qf[0], qf[1]], axis=0))
    for d in range(27):
        one_out[d] = turned[4 * d : 4 * d + 4, :]

    for k, ref in enumerate((fine, pool, grad2)):
        halo_sent(k, ref)
    to_pair(0, ga.at[other], ra).wait_send()
    to_pair(1, qs, qra).wait_send()
    to_pair(2, fd.at[core], fd.at[core]).wait_send()
    to_pair(3, qf.at[core], qf.at[core]).wait_send()
    for off in line:
        to_line(0, off, sb.at[on_line(off)], rb.at[off - 1]).wait_send()
        to_line(1, off, qsc.at[0], qrb.at[iz]).wait_send()
        to_line(2, off, fd.at[core, iz], fd.at[core, iz]).wait_send()
    for off in flat:
        to_plane(0, off, sc, rc.at[me_plane]).wait_send()
        to_plane(1, off, qsc.at[1], qrc.at[me_plane]).wait_send()
    for k, (half, out) in enumerate(((half1, acts_out), (half2, grads_out))):
        here, there = out_copies(k, half, out)
        here.wait()
        there.wait()


def solution(mesh):
    nd, nz, ny = mesh.shape["dp"], mesh.shape["gz"], mesh.shape["gy"]
    plane = nd * ny

    def per_device(volumes, conv_one, conv_two, cotangent):
        micro, feats, sz, sy, sx = volumes.shape
        rows = sz * sy
        dims = (nd, nz, ny, sz, sy, micro * nd)
        vol = volumes.reshape(micro, feats * rows, sx)
        one = conv_one.transpose(2, 3, 4, 1, 0).reshape(27, 4, 32)
        two = conv_two.transpose(2, 3, 4, 1, 0).reshape(27, 32, 64)
        cot = cotangent[:, :, 0].transpose(0, 2, 1, 3)
        whole = pl.BlockSpec(memory_space=pltpu.VMEM)
        away = pl.BlockSpec(memory_space=pl.ANY)
        vmem = pltpu.VMEM
        dma = pltpu.SemaphoreType.DMA
        acts, grads, g_one, g_two = pl.pallas_call(
            functools.partial(step_kernel, dims),
            out_shape=(
                jax.ShapeDtypeStruct(vol.shape, BF16),
                jax.ShapeDtypeStruct(vol.shape, BF16),
                jax.ShapeDtypeStruct((27, 4, 32), F32),
                jax.ShapeDtypeStruct((27, 32, 64), F32),
            ),
            in_specs=[away, whole, whole, whole],
            out_specs=(away, away, whole, whole),
            scratch_shapes=[
                vmem((feats * rows, sx), BF16),
                vmem((feats * rows, sx), F32),
                vmem((2 * sz + 2, 2 * sy + 2, 16, sx), BF16),
                vmem((sz + 2, sy + 2, 32, sx), BF16),
                vmem((sz + 2, sy + 2, 64, sx), BF16),
                vmem((sz, sy, 256, sx), F32),
                vmem((sz, sy // 2, 256, 2 * sx), BF16),
                vmem((sy // 2, 64, sx), F32),
                vmem((8, 128, 256), BF16),
                vmem((256, 256), BF16),
                vmem((192, 288), BF16),
                vmem((96, 576), BF16),
                vmem((256, 256), F32),
                vmem((288, 256), F32),
                vmem((32 * rows, sx), F32),
                vmem((32 * rows, sx), F32),
                vmem((32 * rows, sx), BF16),
                vmem((32 * rows, sx), BF16),
                vmem((2, 8, 32, 128), F32),
                vmem((8, 32, 128), F32),
                vmem((8, 32, 128), F32),
                vmem((max(nz - 1, 1), 32, 128), F32),
                vmem((32, 128), F32),
                vmem((plane, 32, 128), F32),
                vmem((2, 8, 32, 128), F32),
                vmem((1, 128, 128), F32),
                vmem((32, 128), F32),
                vmem((32, 128), F32),
                vmem((nz, 16, 128), F32),
                vmem((2, 16, 128), F32),
                vmem((plane, 16, 128), F32),
                vmem((2, 16, 128), F32),
                dma((3,)), dma((2,)), dma((2,)),
                dma((3, 8)), dma((3, 8)),
                dma((4,)), dma((4,)),
                dma((3, nz - 1)), dma((3, nz - 1)),
                dma((2, plane - 1)), dma((2, plane - 1)),
            ],
            compiler_params=pltpu.CompilerParams(
                collective_id=0, has_side_effects=True, vmem_limit_bytes=48 * 2**20
            ),
        )(vol, one, two, cot)
        g_one = g_one.reshape(3, 3, 3, 4, 32).transpose(4, 3, 0, 1, 2)
        g_two = g_two.reshape(3, 3, 3, 32, 64).transpose(4, 3, 0, 1, 2)
        return acts.reshape(volumes.shape), grads.reshape(volumes.shape), g_one, g_two

    in_specs = (P("dp", None, "gz", "gy", None), P(), P(), P("dp", None, "gz", "gy", None))
    out_specs = (P("dp", None, "gz", "gy", None), P("dp", None, "gz", "gy", None), P(), P())
    return jax.shard_map(per_device, mesh=mesh, in_specs=in_specs, out_specs=out_specs, check_vma=False)
```

time: 625 us -> 57.2 us (0.09); the launches traced: 616 us -> 57 us
  waiting for transfers between devices: 262 us -> 0 us
  local copies, waits for them, and re-layouts: 120 us -> 5.47 us
  blocking collectives: 85.8 us -> 0 us
  matrix products: 60.2 us -> 0 us
  Pallas kernels: 0 us -> 50.9 us
  other arithmetic: 42.4 us -> 0 us
  starting transfers between devices: 31.1 us -> 0 us
  between operations: 15.1 us -> 0.65 us
    psum x1 -> x0, waiting for transfers between devices: 245 us -> none  [per_device(): lax.psum((grad_one, grad_two), ('dp', 'pipe', 'gz', 'gy'))]
    psum x1 -> x0, blocking collectives: 76.9 us -> none  [per_device(): lax.psum((grad_one, grad_two), ('dp', 'pipe', 'gz', 'gy'))]
    pallas_call x0 -> x1, Pallas kernels: none -> 50.9 us  [per_device(): pl.pallas_call(functools.partial(step_kernel, dims), out_shape=(jax.Shape...]
    conv_general_dilated x12 -> x0, local copies, waits for them, and re-layouts: 43.1 us -> none  [convolve_valid(): lax.conv_general_dilated(pad_width(grid_in)[None], kernel, (1, 1, 1), 'VA...]
    ppermute x12 -> x0, starting transfers between devices: 31 us -> none  [the longest x6 23.3 us: padded_2(): lax.ppermute(tail, axis, [(i, (i + 1) % count) for i in range(ends)])]
    dot_general x54 -> x0, matrix products: 30.5 us -> none  [kernel_grad(): jnp.einsum('op,cp->oc', flat_out, shifted, preferred_element_type=jnp.flo...]
    conv_general_dilated x3 -> x0, matrix products: 29.7 us -> none  [convolve_valid(): lax.conv_general_dilated(pad_width(grid_in)[None], kernel, (1, 1, 1), 'VA...]
    div x10 -> x0, local copies, waits for them, and re-layouts: 28.9 us -> none  [the longest x4 22.7 us: derivative(): return LEAK_SLOPE + (1.0 - LEAK_SLOPE) * jax.nn.sigmoid(pre_act)]
  transfers between devices with their start and end apart: 13 -> 0, of which waited for: 6 -> 0; matrix products, arithmetic and copies ran while one was open for 4% -> 0% of each run, Pallas kernels for 0% -> 0%
where the time goes in v1:
time: 57.2 us; the launch traced here: 57 us
  Pallas kernels  50.9 us (89%)
  local copies, waits for them, and re-layouts  5.47 us (10%)
  between operations  0.65 us (1%)
    pallas_call x1, Pallas kernels, per_device(): pl.pallas_call(functools.partial(step_kernel, dims), out_shape=(jax.Shape...  50.9 us
    unnamed x11, local copies, waits for them, and re-layouts  5.47 us

profile of v1, /device:TPU:1, one launch (start us, length us, event | category | flops | bytes accessed | tf_op | source)
XLA Modules:
  0.0 57.0 jit_solution(11481444871461992512)
XLA Ops:
  0.6 0.0 copy-start
  0.6 1.0 %copy.10 = bf16[2,64,1,4,64]{4,1,3,0,2:T(8,128)(2,1)S(1)} copy(bf16[2,64,1,4,64]{4,3,2,1,0:T(4,128)(2,1)} %param.7) | data formatting | bytes 131072 | tf_op args[3]
  1.6 0.0 copy-done
  1.6 0.0 copy-start.1
  1.6 0.9 %copy-done.1 = bf16[64,32,3,3,3]{0,1,4,3,2:T(8,128)(2,1)S(1)} copy-done((bf16[64,32,3,3,3]{0,1,4,3,2:T(8,128)(2,1)S(1)}, bf16[64,32,3,3,3]{0,1,4,3,2:T(8,128)(2,1)}, u32[]{:S(2)}) %copy-start.1) | copy-done | bytes 110616
  2.6 0.0 copy-start.2
  2.6 0.7 %copy-done.2 = bf16[32,4,3,3,3]{0,1,4,3,2:T(4,128)(2,1)S(1)} copy-done((bf16[32,4,3,3,3]{0,1,4,3,2:T(4,128)(2,1)S(1)}, bf16[32,4,3,3,3]{0,1,4,3,2:T(4,128)(2,1)}, u32[]{:S(2)}) %copy-start.2) | copy-done | bytes 6936
  3.3 50.9 %shard_map.75 = (bf16[2,512,128]{2,1,0:T(8,128)(2,1)S(1)}, bf16[2,512,128]{2,1,0:T(8,128)(2,1)S(1)}, f32[27,4,32]{2,1,0:T(4,128)S(1)}, f32[27,32,64]{2,1,0:T(8,128)S(1)}) custom-call(bf16[2,512,128]{2,1,0:T(8,128)(2,1)S(1)} %bitcast.22, bf16[27,4,32]{2,1,0:T(4,128)(2,1)S(1)} %bitcast.27, bf16[27,32,64]{2,1,0:T(8,128)(2,1)S(1)} %bitcast.25, ...), custom_call_target="tpu_custom_call" | custom-call | tf_op jit(solution)/shard_map/pallas_call | solution.py:486
  54.2 0.7 %copy.15 = bf16[2,32,2,8,128]{4,3,2,1,0:T(8,128)(2,1)} copy(bf16[2,32,2,8,128]{4,3,2,1,0:T(8,128)(2,1)S(1)} %bitcast.24) | data formatting | bytes 524288
  54.9 0.7 %copy.16 = bf16[2,32,2,8,128]{4,3,2,1,0:T(8,128)(2,1)} copy(bf16[2,32,2,8,128]{4,3,2,1,0:T(8,128)(2,1)S(1)} %bitcast.23) | data formatting | bytes 524288
  55.6 0.6 %copy.17 = f32[32,4,3,3,3]{0,1,4,3,2:T(4,128)} copy(f32[32,4,3,3,3]{0,1,4,3,2:T(4,128)S(1)} %bitcast.26) | data formatting | bytes 27648
  56.3 0.8 %copy.18 = f32[64,32,3,3,3]{0,1,4,3,2:T(8,128)} copy(f32[64,32,3,3,3]{0,1,4,3,2:T(8,128)S(1)} %bitcast.21) | data formatting | bytes 442368
Async XLA Ops:
  0.6 1.0 %copy-start = (bf16[2,32,2,8,128]{4,3,2,1,0:T(8,128)(2,1)S(1)}, bf16[2,32,2,8,128]{4,3,2,1,0:T(8,128)(2,1)}, u32[]{:S(2)}) copy-start(bf16[2,32,2,8,128]{4,3,2,1,0:T(8,128)(2,1)} %param.4) | copy-start | bytes 786436
  1.6 0.9 %copy-start.1 = (bf16[64,32,3,3,3]{0,1,4,3,2:T(8,128)(2,1)S(1)}, bf16[64,32,3,3,3]{0,1,4,3,2:T(8,128)(2,1)}, u32[]{:S(2)}) copy-start(bf16[64,32,3,3,3]{0,1,4,3,2:T(8,128)(2,1)} %param.6) | copy-start | bytes 331780
  2.6 0.7 %copy-start.2 = (bf16[32,4,3,3,3]{0,1,4,3,2:T(4,128)(2,1)S(1)}, bf16[32,4,3,3,3]{0,1,4,3,2:T(4,128)(2,1)}, u32[]{:S(2)}) copy-start(bf16[32,4,3,3,3]{0,1,4,3,2:T(4,128)(2,1)} %param.5) | copy-start | bytes 20740

commit v2 on v1

--- a/solution.py
+++ b/solution.py
@@ -63,9 +63,9 @@
 
 def step_kernel(
     dims,
-    vol, one_ref, two_ref, cot_ref,
+    vol, one_in, two_in, cot_in,
     acts_out, grads_out, one_out, two_out,
-    raw, rawf, fine, pool, grad2, slope1, shifted, cots, sel, w1, w2, wb,
+    one_ref, two_ref, cot_ref, cotf, raw, rawf, fine, pool, grad2, slope1, shifted, cots, sel, w1, w2, wb,
     sum1, sum2, flat1, flat2, half1, half2,
     ga, ra, sb, rb, sc, rc, fd,
     qa, qra, qs, qrb, qsc, qrc, qf,
@@ -166,6 +166,12 @@
 
     fetch = pltpu.make_async_copy(vol.at[core], raw, local_sem.at[0])
     fetch.start()
+    fetch_more = [
+        pltpu.make_async_copy(src, dst, local_sem.at[3 + k])
+        for k, (src, dst) in enumerate(((one_in, one_ref), (two_in, two_ref), (cot_in.at[core], cot_ref)))
+    ]
+    for copy in fetch_more:
+        copy.start()
     barrier = pltpu.get_barrier_semaphore()
     pl.semaphore_signal(barrier, inc=1, device_id={"pipe": other}, device_id_type=MESH)
     count = jnp.int32(1 + (nz - 1) + (plane - 1))
@@ -207,7 +213,7 @@
                 body(z, y)
                 return 0
 
-            lax.fori_loop(0, sy, inner, 0)
+            lax.fori_loop(0, sy, inner, 0, unroll=4)
             return 0
 
         lax.fori_loop(0, sz, outer, 0)
@@ -217,12 +223,14 @@
             body(z, p)
             return 0
 
-        lax.fori_loop(0, sy // 2, inner, 0)
+        lax.fori_loop(0, sy // 2, inner, 0, unroll=True)
 
     loop_rows(spread_row)
     pl.semaphore_wait(barrier, count)
     halo_send(0, fine)
 
+    for copy in fetch_more:
+        copy.wait()
     row = lax.broadcasted_iota(jnp.int32, (128, 256), 0)
     lane = lax.broadcasted_iota(jnp.int32, (128, 256), 1)
     tap = row >> 2
@@ -254,8 +262,11 @@
         (lax.broadcasted_iota(jnp.int32, (64, LANES), 1) >> 1)
         == lax.broadcasted_iota(jnp.int32, (64, LANES), 0)
     ).astype(BF16)
+    for o in range(64):
+        cotf[4 * o : 4 * o + 4, 0:64] = cot_ref[o].astype(F32)
     for y in range(sy // 2):
-        cots[y] = mm(cot_ref[core, y], double) * 0.125
+        mine = cotf[pl.ds(y, 64, stride=sy // 2), :]
+        cots[y] = mm(mine[:, 0:64].astype(BF16), double) * 0.125
 
     def windows(z, p):
         return jnp.concatenate(
@@ -467,6 +478,15 @@
         there.wait()
 
 
+def leave_kernel(*refs):
+    sem = refs[8]
+    copies = [pltpu.make_async_copy(refs[k], refs[4 + k], sem.at[k]) for k in range(4)]
+    for copy in copies:
+        copy.start()
+    for copy in copies:
+        copy.wait()
+
+
 def solution(mesh):
     nd, nz, ny = mesh.shape["dp"], mesh.shape["gz"], mesh.shape["gy"]
     plane = nd * ny
@@ -478,22 +498,22 @@
         vol = volumes.reshape(micro, feats * rows, sx)
         one = conv_one.transpose(2, 3, 4, 1, 0).reshape(27, 4, 32)
         two = conv_two.transpose(2, 3, 4, 1, 0).reshape(27, 32, 64)
-        cot = cotangent[:, :, 0].transpose(0, 2, 1, 3)
+        cot = cotangent[:, :, 0]
         whole = pl.BlockSpec(memory_space=pltpu.VMEM)
-        away = pl.BlockSpec(memory_space=pl.ANY)
+        away = pl.BlockSpec(memory_space=pltpu.HBM)
         vmem = pltpu.VMEM
         dma = pltpu.SemaphoreType.DMA
-        acts, grads, g_one, g_two = pl.pallas_call(
+        results = ((vol.shape, BF16), (vol.shape, BF16), ((27, 4, 32), F32), ((27, 32, 64), F32))
+        held = pl.pallas_call(
             functools.partial(step_kernel, dims),
-            out_shape=(
-                jax.ShapeDtypeStruct(vol.shape, BF16),
-                jax.ShapeDtypeStruct(vol.shape, BF16),
-                jax.ShapeDtypeStruct((27, 4, 32), F32),
-                jax.ShapeDtypeStruct((27, 32, 64), F32),
-            ),
-            in_specs=[away, whole, whole, whole],
-            out_specs=(away, away, whole, whole),
+            out_shape=tuple(vmem(shape, dtype) for shape, dtype in results),
+            in_specs=[away] * 4,
+            out_specs=(whole,) * 4,
             scratch_shapes=[
+                vmem((27, 4, 32), BF16),
+                vmem((27, 32, 64), BF16),
+                vmem((64, sy // 2, 64), BF16),
+                vmem((64 * (sy // 2), LANES), F32),
                 vmem((feats * rows, sx), BF16),
                 vmem((feats * rows, sx), F32),
                 vmem((2 * sz + 2, 2 * sy + 2, 16, sx), BF16),
@@ -526,7 +546,7 @@
                 vmem((2, 16, 128), F32),
                 vmem((plane, 16, 128), F32),
                 vmem((2, 16, 128), F32),
-                dma((3,)), dma((2,)), dma((2,)),
+                dma((6,)), dma((2,)), dma((2,)),
                 dma((3, 8)), dma((3, 8)),
                 dma((4,)), dma((4,)),
                 dma((3, nz - 1)), dma((3, nz - 1)),
@@ -535,7 +555,14 @@
             compiler_params=pltpu.CompilerParams(
                 collective_id=0, has_side_effects=True, vmem_limit_bytes=48 * 2**20
             ),
-        )(vol, one, two, cot)
+        )(*(pltpu.with_memory_space_constraint(a, pltpu.HBM) for a in (vol, one, two, cot)))
+        acts, grads, g_one, g_two = pl.pallas_call(
+            leave_kernel,
+            out_shape=tuple(jax.ShapeDtypeStruct(shape, dtype) for shape, dtype in results),
+            in_specs=[whole] * 4,
+            out_specs=(away,) * 4,
+            scratch_shapes=[dma((4,))],
+        )(*(pltpu.with_memory_space_constraint(a, pltpu.VMEM) for a in held))
         g_one = g_one.reshape(3, 3, 3, 4, 32).transpose(4, 3, 0, 1, 2)
         g_two = g_two.reshape(3, 3, 3, 32, 64).transpose(4, 3, 0, 1, 2)
         return acts.reshape(volumes.shape), grads.reshape(volumes.shape), g_one, g_two

time: 57.2 us -> 49.2 us (0.86)
  local copies, waits for them, and re-layouts: 5.47 us -> 0 us
  Pallas kernels: 50.9 us -> 48.5 us
    unnamed x11 -> x0, local copies, waits for them, and re-layouts: 5.47 us -> none
    pallas_call x1 -> x2, Pallas kernels: 50.9 us -> 48.5 us  [the longest x1 47.5 us: per_device(): pl.pallas_call(functools.partial(step_kernel, dims), out_shape=tuple((vme...]
where the time goes in v2:
time: 49.2 us; the launch traced here: 49.1 us
  Pallas kernels  48.5 us (99%)
  between operations  0.64 us (1%)
    pallas_call x1, Pallas kernels, per_device(): pl.pallas_call(functools.partial(step_kernel, dims), out_shape=tuple((vme...  47.5 us
    pallas_call x1, Pallas kernels, per_device(): pl.pallas_call(leave_kernel, out_shape=tuple((jax.ShapeDtypeStruct(shape,...  0.99 us

profile of v2, /device:TPU:1, one launch (start us, length us, event | category | flops | bytes accessed | tf_op | source)
XLA Modules:
  0.0 49.1 jit_solution(3166987734599794207)
XLA Ops:
  0.6 47.5 %shard_map.75 = (bf16[2,512,128]{2,1,0:T(8,128)(2,1)S(1)}, bf16[2,512,128]{2,1,0:T(8,128)(2,1)S(1)}, f32[27,4,32]{2,1,0:T(4,128)S(1)}, f32[27,32,64]{2,1,0:T(8,128)S(1)}) custom-call(bf16[2,512,128]{2,1,0:T(8,128)(2,1)} %bitcast.16, bf16[27,4,32]{2,1,0:T(4,128)(2,1)} %bitcast.19, bf16[27,32,64]{2,1,0:T(8,128)(2,1)} %bitcast.17, bf16[2,64,4,64]{3,2,1,0:T(4,128)(2,1)} %bitcast.18), custom_call_target="tpu_custom_call" | custom-call | tf_op jit(solution)/shard_map/pallas_call | solution.py:507
  48.1 1.0 %shard_map.76 = (bf16[2,512,128]{2,1,0:T(8,128)(2,1)}, bf16[2,512,128]{2,1,0:T(8,128)(2,1)}, f32[27,4,32]{2,1,0:T(4,128)}, f32[27,32,64]{2,1,0:T(8,128)}) custom-call(bf16[2,512,128]{2,1,0:T(8,128)(2,1)S(1)} %get-tuple-element.12.refs_0_, bf16[2,512,128]{2,1,0:T(8,128)(2,1)S(1)} %get-tuple-element.13.refs_1_, f32[27,4,32]{2,1,0:T(4,128)S(1)} %get-tuple-element.14.refs_2_, ...), custom_call_target="tpu_custom_call" | custom-call | tf_op jit(solution)/shard_map/pallas_call | solution.py:559

commit v3 on v2

--- a/solution.py
+++ b/solution.py
@@ -43,14 +43,7 @@
 
 
 def slope_of(v):
-    return LEAK + REST / (1.0 + jnp.exp(-v))
-
-
-def act_and_slope(v):
-    e = jnp.exp(-jnp.abs(v))
-    r = 1.0 / (1.0 + e)
-    act = LEAK * v + REST * (jnp.maximum(v, 0.0) + jnp.log(1.0 + e) - LOG_TWO)
-    return act, LEAK + REST * jnp.where(v >= 0.0, r, e * r)
+    return (LEAK + 0.5 * REST) + (0.5 * REST) * jnp.tanh(0.5 * v)
 
 
 def part(d, n):
@@ -71,7 +64,7 @@
     qa, qra, qs, qrb, qsc, qrc, qf,
     local_sem, out_ssem, out_rsem,
     h_ssem, h_rsem,
-    pair_ssem, pair_rsem, line_ssem, line_rsem, plane_ssem, plane_rsem,
+    word_sem, pair_ssem, pair_rsem, line_ssem, line_rsem, plane_ssem, plane_rsem,
 ):
     nd, nz, ny, sz, sy, batch = dims
     rows = sz * sy
@@ -115,6 +108,50 @@
             device_id_type=MESH,
         )
 
+    turns = tuple(
+        (p, dz, dy)
+        for p in range(sz)
+        for dz in (-1, 0, 1)
+        for dy in (-1, 0, 1)
+        if (dz, dy) != (0, 0) and (dz == 0 or p == (0 if dz == -1 else sz - 1))
+    )
+
+    def plane_copy(k, ref, m):
+        p, dz, dy = turns[m]
+        fy, ty = part(dy, ref.shape[1] - 2)
+        to_z = p + 1 if dz == 0 else (0 if dz == 1 else sz + 1)
+        return pltpu.make_async_remote_copy(
+            src_ref=ref.at[p + 1, fy],
+            dst_ref=ref.at[to_z, ty],
+            send_sem=h_ssem.at[k, m],
+            recv_sem=h_rsem.at[k, m],
+            device_id=neighbour(dz, dy),
+            device_id_type=MESH,
+        )
+
+    def plane_send(k, ref, p):
+        for m, (q, dz, dy) in enumerate(turns):
+            if q == p:
+
+                @pl.when(exists(dz, dy))
+                def _():
+                    plane_copy(k, ref, m).start()
+
+    def plane_arrive(k, ref, wanted):
+        for m, (q, dz, dy) in enumerate(turns):
+            if dz in wanted:
+
+                @pl.when(exists(-dz, -dy))
+                def _():
+                    plane_copy(k, ref, m).wait_recv()
+
+    def planes_sent(k, ref):
+        for m, (q, dz, dy) in enumerate(turns):
+
+            @pl.when(exists(dz, dy))
+            def _():
+                plane_copy(k, ref, m).wait_send()
+
     def halo_clear(ref):
         for dz, dy in DIRS:
             _, tz = part(dz, ref.shape[0] - 2)
@@ -174,7 +211,14 @@
         copy.start()
     barrier = pltpu.get_barrier_semaphore()
     pl.semaphore_signal(barrier, inc=1, device_id={"pipe": other}, device_id_type=MESH)
-    count = jnp.int32(1 + (nz - 1) + (plane - 1))
+    near = [
+        {axis: lax.rem(at + step, size)}
+        for axis, at, size in (("gz", iz, nz), ("gy", iy, ny), ("dp", idp, nd))
+        for step in (1, size - 1)
+    ]
+    count = jnp.int32(1 + len(near))
+    for there in near:
+        pl.semaphore_signal(barrier, inc=1, device_id=there, device_id_type=MESH)
     for dz, dy in DIRS:
         if dz != 0 and dy != 0:
 
@@ -183,10 +227,13 @@
                 pl.semaphore_signal(barrier, inc=1, device_id=neighbour(dz, dy), device_id_type=MESH)
 
             count = count + exists(dz, dy).astype(jnp.int32)
-    for off in range(1, plane):
-        pl.semaphore_signal(barrier, inc=1, device_id=on_plane(off)[1], device_id_type=MESH)
-    for off in range(1, nz):
-        pl.semaphore_signal(barrier, inc=1, device_id={"gz": on_line(off)}, device_id_type=MESH)
+
+    def spread_word(r):
+        for there in near:
+            pl.semaphore_signal(word_sem.at[r], inc=1, device_id=there, device_id_type=MESH)
+
+    def hear_word(r):
+        pl.semaphore_wait(word_sem.at[r], len(near))
 
     halo_clear(fine)
     halo_clear(pool)
@@ -218,16 +265,24 @@
 
         lax.fori_loop(0, sz, outer, 0)
 
-    def loop_pairs(z, body):
-        def inner(p, _):
+    def loop_pairs(z, body, first=0, last=sy // 2):
+        for p in range(first, last):
             body(z, p)
-            return 0
-
-        lax.fori_loop(0, sy // 2, inner, 0, unroll=True)
+
+    up, down = tuple(range(sz)), tuple(reversed(range(sz)))
+
+    def needs(order, z):
+        wanted = () if z != order[0] else (0,)
+        if z == 0:
+            wanted += (1,)
+        if z == sz - 1:
+            wanted += (-1,)
+        return wanted
 
     loop_rows(spread_row)
     pl.semaphore_wait(barrier, count)
     halo_send(0, fine)
+    spread_word(0)
 
     for copy in fetch_more:
         copy.wait()
@@ -277,19 +332,25 @@
         pre = mm(w1[...], windows(z, p))
         for j in range(2):
             y = 2 * p + j
-            total = jnp.zeros((32, LANES), F32)
+            straight, product = None, None
             for s in range(8):
-                act, slope = act_and_slope(pre[32 * s : 32 * s + 32, LANES * j : LANES * j + LANES])
-                total = total + act
-                slope1[z, y, 32 * s : 32 * s + 32, :] = slope
-            mean = total * 0.125
+                v = pre[32 * s : 32 * s + 32, LANES * j : LANES * j + LANES]
+                slope1[z, y, 32 * s : 32 * s + 32, :] = slope_of(v)
+                bend, grown = jnp.maximum(v, LEAK * v), 1.0 + jnp.exp(-jnp.abs(v))
+                straight = bend if s == 0 else straight + bend
+                product = grown if s == 0 else product * grown
+            mean = 0.125 * straight + (0.125 * REST) * jnp.log(product) - REST * LOG_TWO
             pool[z + 1, y + 1] = mean.astype(BF16)
             flat1[pl.ds(z * sy + y, 32, stride=rows), :] = mean
 
+    hear_word(0)
+    spread_word(1)
     halo_arrive(0, fine)
-    for z in range(sz):
+    for z in up:
         loop_pairs(z, first_pair)
-    halo_send(1, pool)
+        plane_send(1, pool, z)
+    hear_word(1)
+    spread_word(2)
     half1[...] = flat1[...].astype(BF16)
 
     def out_copies(k, half, out):
@@ -321,10 +382,10 @@
             shifted[z, p, 128:192, cols] = right
             shifted[z, p, 192:256, cols] = right
 
-    halo_arrive(1, pool)
-    for z in range(sz):
+    for z in down:
+        plane_arrive(1, pool, needs(down, z))
         loop_pairs(z, second_pair)
-    halo_send(2, grad2)
+        plane_send(2, grad2, z)
 
     sum2[...] = jnp.zeros(sum2.shape, F32)
 
@@ -336,16 +397,14 @@
 
     for z in range(sz):
         loop_pairs(z, second_terms)
-    for r in range(9):
-        ga[r // 8, r % 8] = sum2[32 * r : 32 * r + 32, 0:128]
+    for r in range(18):
+        ga[r // 16, r % 16] = sum2[16 * r : 16 * r + 16, 0:128]
     keep = lax.broadcasted_iota(jnp.int32, (16, LANES), 1) < 64
     for r in range(9):
         lo, hi = sum2[16 * r : 16 * r + 16, 128:256], sum2[144 + 16 * r : 160 + 16 * r, 128:256]
-        at = 288 + 16 * r
-        ga[at // 256, at % 256 // 32, at % 32 : at % 32 + 16] = jnp.where(keep, lo, hi)
-    ga[1, 5, 16:32] = jnp.zeros((16, LANES), F32)
-    ga[1, 6] = jnp.zeros((32, LANES), F32)
-    ga[1, 7] = jnp.zeros((32, LANES), F32)
+        ga[1, 2 + r] = jnp.where(keep, lo, hi)
+    for r in range(11, 16):
+        ga[1, r] = jnp.zeros((16, LANES), F32)
     to_pair(0, ga.at[other], ra).start()
 
     sum1[...] = jnp.zeros(sum1.shape, F32)
@@ -373,105 +432,106 @@
     line = range(1, nz)
     flat = range(1, plane)
 
-    halo_arrive(2, grad2)
-    loop_pairs(0, back_pair)
+    hear_word(2)
     to_pair(0, ga.at[other], ra).wait_recv()
-    for j in range(8):
-        sb[j] = ga[core, j] + ra[j]
-    for off in line:
-        to_line(0, off, sb.at[on_line(off)], rb.at[off - 1]).start()
-    for z in range(1, sz):
+    sb[...] = ga[core] + ra[...]
+    for off in flat:
+        to_plane(0, off, sb.at[on_plane(off)[0]], rb.at[off - 1]).start()
+    for z in up:
+        plane_arrive(2, grad2, needs(up, z))
         loop_pairs(z, back_pair)
 
-    folded = jnp.zeros((32, LANES), F32)
+    pieces = []
     for s in range(8):
         mine = sum1[32 * s : 32 * s + 32, :]
         high = mine.astype(BF16)
         low = (mine - high.astype(F32)).astype(BF16)
-        folded = folded + mm_nt(high, sel[s]) + mm_nt(low, sel[s])
-    qs[...] = folded
+        pieces.append(jnp.concatenate([high, low], axis=0))
+    folded = mm_nt(jnp.concatenate(pieces, axis=1), jnp.concatenate([sel[s] for s in range(8)], axis=1))
+    qs[...] = folded[0:32] + folded[32:64]
     to_pair(1, qs, qra).start()
-    half2[...] = flat2[...].astype(BF16)
-    for copy in out_copies(1, half2, grads_out):
-        copy.start()
-
-    for off in line:
-        to_line(0, off, sb.at[on_line(off)], rb.at[off - 1]).wait_recv()
-    total = sb[iz]
-    for off in line:
+
+    for off in flat:
+        to_plane(0, off, sb.at[on_plane(off)[0]], rb.at[off - 1]).wait_recv()
+    total = sb[me_plane]
+    for off in flat:
         total = total + rb[off - 1]
     sc[...] = total
-    rc[me_plane] = total
-    for off in flat:
-        to_plane(0, off, sc, rc.at[me_plane]).start()
+    rc[iz] = total
+    for off in line:
+        to_line(0, off, sc, rc.at[iz]).start()
 
     to_pair(1, qs, qra).wait_recv()
     both = qs[...] + qra[...]
     mine = jnp.where(core == 0, both[0:16], both[16:32])
     qsc[0] = mine
-    qrb[iz] = mine
+    qrc[me_plane] = mine
+    for off in flat:
+        to_plane(1, off, qsc.at[0], qrc.at[me_plane]).start()
+    half2[...] = flat2[...].astype(BF16)
+    for copy in out_copies(1, half2, grads_out):
+        copy.start()
+
+    for off in flat:
+        to_plane(1, off, qsc.at[0], qrc.at[me_plane]).wait_recv()
+    total = qrc[0]
+    for q in range(1, plane):
+        total = total + qrc[q]
+    qsc[1] = total
+    qrb[iz] = total
     for off in line:
-        to_line(1, off, qsc.at[0], qrb.at[iz]).start()
-
-    for off in flat:
-        to_plane(0, off, sc, rc.at[me_plane]).wait_recv()
+        to_line(1, off, qsc.at[1], qrb.at[iz]).start()
+
+    for off in line:
+        to_line(0, off, sc, rc.at[iz]).wait_recv()
     total = rc[0]
-    for q in range(1, plane):
+    for q in range(1, nz):
         total = total + rc[q]
-    fd[core, iz] = total * (1.0 / batch)
+    fd[core, me_plane] = total * (1.0 / batch)
+    for off in flat:
+        to_plane(2, off, fd.at[core, me_plane], fd.at[core, me_plane]).start()
+
     for off in line:
-        to_line(2, off, fd.at[core, iz], fd.at[core, iz]).start()
-
-    for off in line:
-        to_line(1, off, qsc.at[0], qrb.at[iz]).wait_recv()
+        to_line(1, off, qsc.at[1], qrb.at[iz]).wait_recv()
     total = qrb[0]
     for q in range(1, nz):
         total = total + qrb[q]
-    qsc[1] = total
-    qrc[me_plane] = total
-    for off in flat:
-        to_plane(1, off, qsc.at[1], qrc.at[me_plane]).start()
-
-    for off in line:
-        to_line(2, off, fd.at[core, iz], fd.at[core, iz]).wait_recv()
-    to_pair(2, fd.at[core], fd.at[core]).start()
-
-    for off in flat:
-        to_plane(1, off, qsc.at[1], qrc.at[me_plane]).wait_recv()
-    total = qrc[0]
-    for q in range(1, plane):
-        total = total + qrc[q]
     qf[core] = total * (1.0 / batch)
     to_pair(3, qf.at[core], qf.at[core]).start()
 
-    to_pair(2, fd.at[core], fd.at[core]).wait_recv()
-    for j in range(9):
-        block = fd[j // 8, j % 8]
-        two_out[3 * j] = block[:, 0:64]
-        two_out[3 * j + 1] = pltpu.roll(block, 64, axis=1)[:, 0:64]
-    for r in range(9):
-        at = 288 + 16 * r
-        block = fd[at // 256, at % 256 // 32, at % 32 : at % 32 + 16]
-        for first, values in ((16 * r, block), (144 + 16 * r, pltpu.roll(block, 64, axis=1))):
-            two_out[3 * (first // 32) + 2, first % 32 : first % 32 + 16, :] = values[:, 0:64]
+    for off in flat:
+        to_plane(2, off, fd.at[core, me_plane], fd.at[core, me_plane]).wait_recv()
+    to_pair(2, fd.at[core], fd.at[core]).start()
+
     to_pair(3, qf.at[core], qf.at[core]).wait_recv()
     turned = jnp.transpose(jnp.concatenate([qf[0], qf[1]], axis=0))
     for d in range(27):
         one_out[d] = turned[4 * d : 4 * d + 4, :]
-
-    for k, ref in enumerate((fine, pool, grad2)):
-        halo_sent(k, ref)
+    to_pair(2, fd.at[core], fd.at[core]).wait_recv()
+    for j in range(18):
+        block = fd[j // 16, j % 16]
+        rows16 = slice(16 * (j % 2), 16 * (j % 2) + 16)
+        two_out[3 * (j // 2), rows16, :] = block[:, 0:64]
+        two_out[3 * (j // 2) + 1, rows16, :] = pltpu.roll(block, 64, axis=1)[:, 0:64]
+    for r in range(9):
+        block = fd[1, 2 + r]
+        for first, values in ((16 * r, block), (144 + 16 * r, pltpu.roll(block, 64, axis=1))):
+            two_out[3 * (first // 32) + 2, first % 32 : first % 32 + 16, :] = values[:, 0:64]
+
+    halo_sent(0, fine)
+    planes_sent(1, pool)
+    planes_sent(2, grad2)
     to_pair(0, ga.at[other], ra).wait_send()
     to_pair(1, qs, qra).wait_send()
     to_pair(2, fd.at[core], fd.at[core]).wait_send()
     to_pair(3, qf.at[core], qf.at[core]).wait_send()
     for off in line:
-        to_line(0, off, sb.at[on_line(off)], rb.at[off - 1]).wait_send()
-        to_line(1, off, qsc.at[0], qrb.at[iz]).wait_send()
-        to_line(2, off, fd.at[core, iz], fd.at[core, iz]).wait_send()
-    for off in flat:
-        to_plane(0, off, sc, rc.at[me_plane]).wait_send()
-        to_plane(1, off, qsc.at[1], qrc.at[me_plane]).wait_send()
+        to_line(0, off, sc, rc.at[iz]).wait_send()
+        to_line(1, off, qsc.at[1], qrb.at[iz]).wait_send()
+    for off in flat:
+        to_plane(0, off, sb.at[on_plane(off)[0]], rb.at[off - 1]).wait_send()
+        to_plane(1, off, qsc.at[0], qrc.at[me_plane]).wait_send()
+        to_plane(2, off, fd.at[core, me_plane], fd.at[core, me_plane]).wait_send()
     for k, (half, out) in enumerate(((half1, acts_out), (half2, grads_out))):
         here, there = out_copies(k, half, out)
         here.wait()
@@ -532,13 +592,13 @@
                 vmem((32 * rows, sx), F32),
                 vmem((32 * rows, sx), BF16),
                 vmem((32 * rows, sx), BF16),
-                vmem((2, 8, 32, 128), F32),
-                vmem((8, 32, 128), F32),
-                vmem((8, 32, 128), F32),
-                vmem((max(nz - 1, 1), 32, 128), F32),
-                vmem((32, 128), F32),
-                vmem((plane, 32, 128), F32),
-                vmem((2, 8, 32, 128), F32),
+                vmem((2, 16, 16, 128), F32),
+                vmem((16, 16, 128), F32),
+                vmem((16, 16, 128), F32),
+                vmem((plane - 1, 16, 128), F32),
+                vmem((16, 128), F32),
+                vmem((nz, 16, 128), F32),
+                vmem((2, 16, 16, 128), F32),
                 vmem((1, 128, 128), F32),
                 vmem((32, 128), F32),
                 vmem((32, 128), F32),
@@ -547,10 +607,10 @@
                 vmem((plane, 16, 128), F32),
                 vmem((2, 16, 128), F32),
                 dma((6,)), dma((2,)), dma((2,)),
-                dma((3, 8)), dma((3, 8)),
-                dma((4,)), dma((4,)),
-                dma((3, nz - 1)), dma((3, nz - 1)),
-                dma((2, plane - 1)), dma((2, plane - 1)),
+                dma((3, 6 + 2 * sz)), dma((3, 6 + 2 * sz)),
+                pltpu.SemaphoreType.REGULAR((3,)), dma((4,)), dma((4,)),
+                dma((2, nz - 1)), dma((2, nz - 1)),
+                dma((3, plane - 1)), dma((3, plane - 1)),
             ],
             compiler_params=pltpu.CompilerParams(
                 collective_id=0, has_side_effects=True, vmem_limit_bytes=48 * 2**20

time: 49.2 us -> 42.9 us (0.87)
  Pallas kernels: 48.5 us -> 42.1 us
    pallas_call x1, Pallas kernels: 47.5 us -> 41.1 us  [per_device(): pl.pallas_call(functools.partial(step_kernel, dims), out_shape=tuple((vme...]
where the time goes in v3:
time: 42.9 us; the launch traced here: 42.8 us
  Pallas kernels  42.1 us (98%)
  between operations  0.64 us (1%)
    pallas_call x1, Pallas kernels, per_device(): pl.pallas_call(functools.partial(step_kernel, dims), out_shape=tuple((vme...  41.1 us
    pallas_call x1, Pallas kernels, per_device(): pl.pallas_call(leave_kernel, out_shape=tuple((jax.ShapeDtypeStruct(shape,...  0.99 us

profile of v3, /device:TPU:1, one launch (start us, length us, event | category | flops | bytes accessed | tf_op | source)
XLA Modules:
  0.0 42.8 jit_solution(15652843536552244141)
XLA Ops:
  0.6 41.1 %shard_map.75 = (bf16[2,512,128]{2,1,0:T(8,128)(2,1)S(1)}, bf16[2,512,128]{2,1,0:T(8,128)(2,1)S(1)}, f32[27,4,32]{2,1,0:T(4,128)S(1)}, f32[27,32,64]{2,1,0:T(8,128)S(1)}) custom-call(bf16[2,512,128]{2,1,0:T(8,128)(2,1)} %bitcast.16, bf16[27,4,32]{2,1,0:T(4,128)(2,1)} %bitcast.19, bf16[27,32,64]{2,1,0:T(8,128)(2,1)} %bitcast.17, bf16[2,64,4,64]{3,2,1,0:T(4,128)(2,1)} %bitcast.18), custom_call_target="tpu_custom_call" | custom-call | tf_op jit(solution)/shard_map/pallas_call | solution.py:567
  41.8 1.0 %shard_map.76 = (bf16[2,512,128]{2,1,0:T(8,128)(2,1)}, bf16[2,512,128]{2,1,0:T(8,128)(2,1)}, f32[27,4,32]{2,1,0:T(4,128)}, f32[27,32,64]{2,1,0:T(8,128)}) custom-call(bf16[2,512,128]{2,1,0:T(8,128)(2,1)S(1)} %get-tuple-element.12.refs_0_, bf16[2,512,128]{2,1,0:T(8,128)(2,1)S(1)} %get-tuple-element.13.refs_1_, f32[27,4,32]{2,1,0:T(4,128)S(1)} %get-tuple-element.14.refs_2_, ...), custom_call_target="tpu_custom_call" | custom-call | tf_op jit(solution)/shard_map/pallas_call | solution.py:619

commit v4 on v3

--- a/solution.py
+++ b/solution.py
@@ -60,11 +60,11 @@
     acts_out, grads_out, one_out, two_out,
     one_ref, two_ref, cot_ref, cotf, raw, rawf, fine, pool, grad2, slope1, shifted, cots, sel, w1, w2, wb,
     sum1, sum2, flat1, flat2, half1, half2,
-    ga, ra, sb, rb, sc, rc, fd,
-    qa, qra, qs, qrb, qsc, qrc, qf,
+    ga, rb, sc, rc, fd,
+    qa, qs, qrb, qsc, qrc,
     local_sem, out_ssem, out_rsem,
     h_ssem, h_rsem,
-    word_sem, pair_ssem, pair_rsem, line_ssem, line_rsem, plane_ssem, plane_rsem,
+    word_sem, line_ssem, line_rsem, plane_ssem, plane_rsem,
 ):
     nd, nz, ny, sz, sy, batch = dims
     rows = sz * sy
@@ -183,22 +183,22 @@
             def _():
                 halo_copy(k, ref, d).wait_send()
 
-    def to_pair(k, src, dst):
+    def to_line(k, off, src, dst, cross=False):
+        there, at = {"gz": on_line(off)}, off - 1
+        if cross:
+            there, at = {**there, "pipe": other}, nz - 1 + off
         return pltpu.make_async_remote_copy(
-            src_ref=src, dst_ref=dst, send_sem=pair_ssem.at[k], recv_sem=pair_rsem.at[k],
-            device_id={"pipe": other}, device_id_type=MESH,
-        )
-
-    def to_line(k, off, src, dst):
+            src_ref=src, dst_ref=dst, send_sem=line_ssem.at[k, at], recv_sem=line_rsem.at[k, at],
+            device_id=there, device_id_type=MESH,
+        )
+
+    def to_plane(k, off, src, dst, cross=False):
+        there, at = on_plane(off)[1], off - 1
+        if cross:
+            there, at = {**there, "pipe": other}, plane - 1 + off
         return pltpu.make_async_remote_copy(
-            src_ref=src, dst_ref=dst, send_sem=line_ssem.at[k, off - 1], recv_sem=line_rsem.at[k, off - 1],
-            device_id={"gz": on_line(off)}, device_id_type=MESH,
-        )
-
-    def to_plane(k, off, src, dst):
-        return pltpu.make_async_remote_copy(
-            src_ref=src, dst_ref=dst, send_sem=plane_ssem.at[k, off - 1], recv_sem=plane_rsem.at[k, off - 1],
-            device_id=on_plane(off)[1], device_id_type=MESH,
+            src_ref=src, dst_ref=dst, send_sem=plane_ssem.at[k, at], recv_sem=plane_rsem.at[k, at],
+            device_id=there, device_id_type=MESH,
         )
 
     fetch = pltpu.make_async_copy(vol.at[core], raw, local_sem.at[0])
@@ -229,11 +229,11 @@
             count = count + exists(dz, dy).astype(jnp.int32)
 
     def spread_word(r):
-        for there in near:
+        for there in (*near, {"pipe": other}):
             pl.semaphore_signal(word_sem.at[r], inc=1, device_id=there, device_id_type=MESH)
 
     def hear_word(r):
-        pl.semaphore_wait(word_sem.at[r], len(near))
+        pl.semaphore_wait(word_sem.at[r], len(near) + 1)
 
     halo_clear(fine)
     halo_clear(pool)
@@ -346,11 +346,13 @@
     hear_word(0)
     spread_word(1)
     halo_arrive(0, fine)
+    hear_word(1)
+    spread_word(2)
     for z in up:
         loop_pairs(z, first_pair)
         plane_send(1, pool, z)
-    hear_word(1)
-    spread_word(2)
+    hear_word(2)
+    spread_word(3)
     half1[...] = flat1[...].astype(BF16)
 
     def out_copies(k, half, out):
@@ -387,27 +389,34 @@
         loop_pairs(z, second_pair)
         plane_send(2, grad2, z)
 
-    sum2[...] = jnp.zeros(sum2.shape, F32)
-
-    def second_terms(z, p):
-        cells = jnp.concatenate(
-            [pool[pl.ds(z, 3), pl.ds(2 * p + j, 3)].reshape(288, LANES) for j in range(2)], axis=1
-        )
-        sum2[...] += mm_nt(cells, shifted[z, p])
-
-    for z in range(sz):
-        loop_pairs(z, second_terms)
+    hear_word(3)
+
+    pieces, sides = [], []
+    for z in up:
+        for y in range(sy):
+            pieces.append(pool[pl.ds(z, 3), pl.ds(y, 3)].reshape(288, LANES))
+        for p in range(sy // 2):
+            sides.append(shifted[z, p])
+    sum2[...] = mm_nt(jnp.concatenate(pieces, axis=1), jnp.concatenate(sides, axis=1))
     for r in range(18):
-        ga[r // 16, r % 16] = sum2[16 * r : 16 * r + 16, 0:128]
+        ga[r // 16, r % 16] = sum2[16 * r : 16 * r + 16, 0:128].astype(BF16)
     keep = lax.broadcasted_iota(jnp.int32, (16, LANES), 1) < 64
     for r in range(9):
         lo, hi = sum2[16 * r : 16 * r + 16, 128:256], sum2[144 + 16 * r : 160 + 16 * r, 128:256]
-        ga[1, 2 + r] = jnp.where(keep, lo, hi)
+        ga[1, 2 + r] = jnp.where(keep, lo, hi).astype(BF16)
     for r in range(11, 16):
-        ga[1, r] = jnp.zeros((16, LANES), F32)
-    to_pair(0, ga.at[other], ra).start()
-
-    sum1[...] = jnp.zeros(sum1.shape, F32)
+        ga[1, r] = jnp.zeros((16, LANES), BF16)
+    slot = core * plane + me_plane
+
+    def scatter(off, cross=False):
+        q = on_plane(off)[0]
+        return to_plane(0, off, ga.at[other if cross else core, q], rb.at[slot], cross)
+
+    rb[slot] = ga[core, me_plane]
+    for off in range(plane):
+        if off > 0:
+            scatter(off).start()
+        scatter(off, True).start()
 
     def back_pair(z, p):
         cells = jnp.concatenate(
@@ -427,19 +436,16 @@
                     [(slope1[z, y, 32 * s : 32 * s + 32, :] * eighth).astype(BF16) for s in range(8)], axis=0
                 )
             )
-        sum1[...] += mm_nt(jnp.concatenate(grads, axis=1), windows(z, p))
+        return jnp.concatenate(grads, axis=1), windows(z, p)
 
     line = range(1, nz)
     flat = range(1, plane)
 
-    hear_word(2)
-    to_pair(0, ga.at[other], ra).wait_recv()
-    sb[...] = ga[core] + ra[...]
-    for off in flat:
-        to_plane(0, off, sb.at[on_plane(off)[0]], rb.at[off - 1]).start()
     for z in up:
         plane_arrive(2, grad2, needs(up, z))
-        loop_pairs(z, back_pair)
+        grads, cells = zip(*(back_pair(z, p) for p in range(sy // 2)))
+        term = mm_nt(jnp.concatenate(grads, axis=1), jnp.concatenate(cells, axis=1))
+        sum1[...] = term if z == up[0] else sum1[...] + term
 
     pieces = []
     for s in range(8):
@@ -448,90 +454,99 @@
         low = (mine - high.astype(F32)).astype(BF16)
         pieces.append(jnp.concatenate([high, low], axis=0))
     folded = mm_nt(jnp.concatenate(pieces, axis=1), jnp.concatenate([sel[s] for s in range(8)], axis=1))
-    qs[...] = folded[0:32] + folded[32:64]
-    to_pair(1, qs, qra).start()
-
-    for off in flat:
-        to_plane(0, off, sb.at[on_plane(off)[0]], rb.at[off - 1]).wait_recv()
-    total = sb[me_plane]
-    for off in flat:
-        total = total + rb[off - 1]
+    folded = (folded[0:32] + folded[32:64]).astype(BF16)
+    qs[0], qs[1] = folded[0:16], folded[16:32]
+    qrc[slot] = qs[core]
+    for off in range(plane):
+        if off > 0:
+            to_plane(1, off, qs.at[core], qrc.at[slot]).start()
+        to_plane(1, off, qs.at[other], qrc.at[slot], True).start()
+
+    for off in range(plane):
+        if off > 0:
+            scatter(off).wait_recv()
+        scatter(off, True).wait_recv()
+    total = rb[0].astype(F32)
+    for q in range(1, 2 * plane):
+        total = total + rb[q].astype(F32)
+    total = total.astype(BF16)
     sc[...] = total
     rc[iz] = total
     for off in line:
         to_line(0, off, sc, rc.at[iz]).start()
-
-    to_pair(1, qs, qra).wait_recv()
-    both = qs[...] + qra[...]
-    mine = jnp.where(core == 0, both[0:16], both[16:32])
-    qsc[0] = mine
-    qrc[me_plane] = mine
-    for off in flat:
-        to_plane(1, off, qsc.at[0], qrc.at[me_plane]).start()
     half2[...] = flat2[...].astype(BF16)
     for copy in out_copies(1, half2, grads_out):
         copy.start()
 
-    for off in flat:
-        to_plane(1, off, qsc.at[0], qrc.at[me_plane]).wait_recv()
-    total = qrc[0]
-    for q in range(1, plane):
-        total = total + qrc[q]
-    qsc[1] = total
-    qrb[iz] = total
-    for off in line:
-        to_line(1, off, qsc.at[1], qrb.at[iz]).start()
+    for off in range(plane):
+        if off > 0:
+            to_plane(1, off, qs.at[core], qrc.at[slot]).wait_recv()
+        to_plane(1, off, qs.at[other], qrc.at[slot], True).wait_recv()
+    total = qrc[0].astype(F32)
+    for q in range(1, 2 * plane):
+        total = total + qrc[q].astype(F32)
+    total = total.astype(BF16)
+    qsc[...] = total
+    qrb[core, iz] = total
+    for off in range(nz):
+        if off > 0:
+            to_line(1, off, qsc, qrb.at[core, iz]).start()
+        to_line(1, off, qsc, qrb.at[core, iz], True).start()
 
     for off in line:
         to_line(0, off, sc, rc.at[iz]).wait_recv()
-    total = rc[0]
+    total = rc[0].astype(F32)
     for q in range(1, nz):
-        total = total + rc[q]
-    fd[core, me_plane] = total * (1.0 / batch)
-    for off in flat:
-        to_plane(2, off, fd.at[core, me_plane], fd.at[core, me_plane]).start()
-
-    for off in line:
-        to_line(1, off, qsc.at[1], qrb.at[iz]).wait_recv()
-    total = qrb[0]
-    for q in range(1, nz):
-        total = total + qrb[q]
-    qf[core] = total * (1.0 / batch)
-    to_pair(3, qf.at[core], qf.at[core]).start()
-
-    for off in flat:
-        to_plane(2, off, fd.at[core, me_plane], fd.at[core, me_plane]).wait_recv()
-    to_pair(2, fd.at[core], fd.at[core]).start()
-
-    to_pair(3, qf.at[core], qf.at[core]).wait_recv()
-    turned = jnp.transpose(jnp.concatenate([qf[0], qf[1]], axis=0))
+        total = total + rc[q].astype(F32)
+    fd[core, me_plane] = (total * (1.0 / batch)).astype(BF16)
+    for off in range(plane):
+        if off > 0:
+            to_plane(2, off, fd.at[core, me_plane], fd.at[core, me_plane]).start()
+        to_plane(2, off, fd.at[core, me_plane], fd.at[core, me_plane], True).start()
+
+    for off in range(nz):
+        if off > 0:
+            to_line(1, off, qsc, qrb.at[core, iz]).wait_recv()
+        to_line(1, off, qsc, qrb.at[core, iz], True).wait_recv()
+    halves = []
+    for half in range(2):
+        total = qrb[half, 0].astype(F32)
+        for q in range(1, nz):
+            total = total + qrb[half, q].astype(F32)
+        halves.append(total * (1.0 / batch))
+    turned = jnp.transpose(jnp.concatenate(halves, axis=0))
     for d in range(27):
         one_out[d] = turned[4 * d : 4 * d + 4, :]
-    to_pair(2, fd.at[core], fd.at[core]).wait_recv()
+    for off in range(plane):
+        if off > 0:
+            to_plane(2, off, fd.at[core, me_plane], fd.at[core, me_plane]).wait_recv()
+        to_plane(2, off, fd.at[core, me_plane], fd.at[core, me_plane], True).wait_recv()
     for j in range(18):
-        block = fd[j // 16, j % 16]
+        block = fd[j // 16, j % 16].astype(F32)
         rows16 = slice(16 * (j % 2), 16 * (j % 2) + 16)
         two_out[3 * (j // 2), rows16, :] = block[:, 0:64]
         two_out[3 * (j // 2) + 1, rows16, :] = pltpu.roll(block, 64, axis=1)[:, 0:64]
     for r in range(9):
-        block = fd[1, 2 + r]
+        block = fd[1, 2 + r].astype(F32)
         for first, values in ((16 * r, block), (144 + 16 * r, pltpu.roll(block, 64, axis=1))):
             two_out[3 * (first // 32) + 2, first % 32 : first % 32 + 16, :] = values[:, 0:64]
 
     halo_sent(0, fine)
     planes_sent(1, pool)
     planes_sent(2, grad2)
-    to_pair(0, ga.at[other], ra).wait_send()
-    to_pair(1, qs, qra).wait_send()
-    to_pair(2, fd.at[core], fd.at[core]).wait_send()
-    to_pair(3, qf.at[core], qf.at[core]).wait_send()
     for off in line:
         to_line(0, off, sc, rc.at[iz]).wait_send()
-        to_line(1, off, qsc.at[1], qrb.at[iz]).wait_send()
+        to_line(1, off, qsc, qrb.at[core, iz]).wait_send()
     for off in flat:
-        to_plane(0, off, sb.at[on_plane(off)[0]], rb.at[off - 1]).wait_send()
-        to_plane(1, off, qsc.at[0], qrc.at[me_plane]).wait_send()
+        scatter(off).wait_send()
+        to_plane(1, off, qs.at[core], qrc.at[slot]).wait_send()
         to_plane(2, off, fd.at[core, me_plane], fd.at[core, me_plane]).wait_send()
+    for off in range(nz):
+        to_line(1, off, qsc, qrb.at[core, iz], True).wait_send()
+    for off in range(plane):
+        scatter(off, True).wait_send()
+        to_plane(1, off, qs.at[other], qrc.at[slot], True).wait_send()
+        to_plane(2, off, fd.at[core, me_plane], fd.at[core, me_plane], True).wait_send()
     for k, (half, out) in enumerate(((half1, acts_out), (half2, grads_out))):
         here, there = out_copies(k, half, out)
         here.wait()
@@ -592,25 +607,21 @@
                 vmem((32 * rows, sx), F32),
                 vmem((32 * rows, sx), BF16),
                 vmem((32 * rows, sx), BF16),
-                vmem((2, 16, 16, 128), F32),
-                vmem((16, 16, 128), F32),
-                vmem((16, 16, 128), F32),
-                vmem((plane - 1, 16, 128), F32),
-                vmem((16, 128), F32),
-                vmem((nz, 16, 128), F32),
-                vmem((2, 16, 16, 128), F32),
+                vmem((2, plane, 16, 128), BF16),
+                vmem((2 * plane, 16, 128), BF16),
+                vmem((16, 128), BF16),
+                vmem((nz, 16, 128), BF16),
+                vmem((2, 16, 16, 128), BF16),
                 vmem((1, 128, 128), F32),
-                vmem((32, 128), F32),
-                vmem((32, 128), F32),
-                vmem((nz, 16, 128), F32),
-                vmem((2, 16, 128), F32),
-                vmem((plane, 16, 128), F32),
-                vmem((2, 16, 128), F32),
+                vmem((2, 16, 128), BF16),
+                vmem((2, nz, 16, 128), BF16),
+                vmem((16, 128), BF16),
+                vmem((2 * plane, 16, 128), BF16),
                 dma((6,)), dma((2,)), dma((2,)),
                 dma((3, 6 + 2 * sz)), dma((3, 6 + 2 * sz)),
-                pltpu.SemaphoreType.REGULAR((3,)), dma((4,)), dma((4,)),
-                dma((2, nz - 1)), dma((2, nz - 1)),
-                dma((3, plane - 1)), dma((3, plane - 1)),
+                pltpu.SemaphoreType.REGULAR((4,)),
+                dma((2, 2 * nz - 1)), dma((2, 2 * nz - 1)),
+                dma((3, 2 * plane - 1)), dma((3, 2 * plane - 1)),
             ],
             compiler_params=pltpu.CompilerParams(
                 collective_id=0, has_side_effects=True, vmem_limit_bytes=48 * 2**20

time: 42.9 us -> 41.7 us (0.972)
  Pallas kernels: 42.1 us -> 41 us
    pallas_call x1, Pallas kernels: 41.1 us -> 40 us  [per_device(): pl.pallas_call(functools.partial(step_kernel, dims), out_shape=tuple((vme...]
where the time goes in v4:
time: 41.7 us; the launch traced here: 41.6 us
  Pallas kernels  41 us (98%)
  between operations  0.64 us (2%)
    pallas_call x1, Pallas kernels, per_device(): pl.pallas_call(functools.partial(step_kernel, dims), out_shape=tuple((vme...  40 us
    pallas_call x1, Pallas kernels, per_device(): pl.pallas_call(leave_kernel, out_shape=tuple((jax.ShapeDtypeStruct(shape,...  0.99 us

profile of v4, /device:TPU:1, one launch (start us, length us, event | category | flops | bytes accessed | tf_op | source)
XLA Modules:
  0.0 41.6 jit_solution(1811107347545431892)
XLA Ops:
  0.6 40.0 %shard_map.75 = (bf16[2,512,128]{2,1,0:T(8,128)(2,1)S(1)}, bf16[2,512,128]{2,1,0:T(8,128)(2,1)S(1)}, f32[27,4,32]{2,1,0:T(4,128)S(1)}, f32[27,32,64]{2,1,0:T(8,128)S(1)}) custom-call(bf16[2,512,128]{2,1,0:T(8,128)(2,1)} %bitcast.16, bf16[27,4,32]{2,1,0:T(4,128)(2,1)} %bitcast.19, bf16[27,32,64]{2,1,0:T(8,128)(2,1)} %bitcast.17, bf16[2,64,4,64]{3,2,1,0:T(4,128)(2,1)} %bitcast.18), custom_call_target="tpu_custom_call" | custom-call | tf_op jit(solution)/shard_map/pallas_call | solution.py:582
  40.7 1.0 %shard_map.76 = (bf16[2,512,128]{2,1,0:T(8,128)(2,1)}, bf16[2,512,128]{2,1,0:T(8,128)(2,1)}, f32[27,4,32]{2,1,0:T(4,128)}, f32[27,32,64]{2,1,0:T(8,128)}) custom-call(bf16[2,512,128]{2,1,0:T(8,128)(2,1)S(1)} %get-tuple-element.12.refs_0_, bf16[2,512,128]{2,1,0:T(8,128)(2,1)S(1)} %get-tuple-element.13.refs_1_, f32[27,4,32]{2,1,0:T(4,128)S(1)} %get-tuple-element.14.refs_2_, ...), custom_call_target="tpu_custom_call" | custom-call | tf_op jit(solution)/shard_map/pallas_call | solution.py:630

commit v5 on v4

--- a/solution.py
+++ b/solution.py
@@ -15,7 +15,7 @@
 F32 = jnp.float32
 BF16 = jnp.bfloat16
 LANES = 128
-DIRS = tuple((dz, dy) for dz in (-1, 0, 1) for dy in (-1, 0, 1) if (dz, dy) != (0, 0))
+DIRS = ((-1, -1), (-1, 1), (1, -1), (1, 1), (0, -1), (0, 1), (-1, 0), (1, 0))
 
 
 def mm(a, b):
@@ -74,6 +74,11 @@
     plane = nd * ny
     me_plane = idp * ny + iy
 
+    ring = lambda off, n: min(off % n, n - off % n)
+    whole_line = sorted(range(nz), key=lambda off: -ring(off, nz))
+    whole_plane = sorted(range(plane), key=lambda off: -ring(off, ny) - ring(off // ny, nd))
+    line, flat = [off for off in whole_line if off], [off for off in whole_plane if off]
+
     def on_line(off):
         return lax.rem(iz + off, nz)
 
@@ -111,9 +116,8 @@
     turns = tuple(
         (p, dz, dy)
         for p in range(sz)
-        for dz in (-1, 0, 1)
-        for dy in (-1, 0, 1)
-        if (dz, dy) != (0, 0) and (dz == 0 or p == (0 if dz == -1 else sz - 1))
+        for dz, dy in DIRS
+        if dz == 0 or p == (0 if dz == -1 else sz - 1)
     )
 
     def plane_copy(k, ref, m):
@@ -335,7 +339,7 @@
             straight, product = None, None
             for s in range(8):
                 v = pre[32 * s : 32 * s + 32, LANES * j : LANES * j + LANES]
-                slope1[z, y, 32 * s : 32 * s + 32, :] = slope_of(v)
+                slope1[z, y, 32 * s : 32 * s + 32, :] = v
                 bend, grown = jnp.maximum(v, LEAK * v), 1.0 + jnp.exp(-jnp.abs(v))
                 straight = bend if s == 0 else straight + bend
                 product = grown if s == 0 else product * grown
@@ -354,6 +358,9 @@
     hear_word(2)
     spread_word(3)
     half1[...] = flat1[...].astype(BF16)
+    for z in range(sz):
+        for y in range(sy):
+            slope1[z, y] = slope_of(slope1[z, y])
 
     def out_copies(k, half, out):
         here = pltpu.make_async_copy(half, out.at[core], local_sem.at[1 + k])
@@ -374,8 +381,11 @@
         for j in range(2):
             mine = prod[:, LANES * j : LANES * j + LANES]
             pre = to_right(mine[0:64]) + mine[64:128] + to_left(mine[128:192])
-            g = (slope_of(pre) * cots[p]).astype(BF16)
-            grad2[z + 1, 2 * p + j + 1] = g
+            grad2[z + 1, 2 * p + j + 1] = (slope_of(pre) * cots[p]).astype(BF16)
+
+    def shift_pair(z, p):
+        for j in range(2):
+            g = grad2[z + 1, 2 * p + j + 1]
             wide = g.astype(F32)
             right = to_right(wide).astype(BF16)
             cols = slice(LANES * j, LANES * j + LANES)
@@ -396,6 +406,7 @@
         for y in range(sy):
             pieces.append(pool[pl.ds(z, 3), pl.ds(y, 3)].reshape(288, LANES))
         for p in range(sy // 2):
+            shift_pair(z, p)
             sides.append(shifted[z, p])
     sum2[...] = mm_nt(jnp.concatenate(pieces, axis=1), jnp.concatenate(sides, axis=1))
     for r in range(18):
@@ -413,7 +424,7 @@
         return to_plane(0, off, ga.at[other if cross else core, q], rb.at[slot], cross)
 
     rb[slot] = ga[core, me_plane]
-    for off in range(plane):
+    for off in whole_plane:
         if off > 0:
             scatter(off).start()
         scatter(off, True).start()
@@ -438,8 +449,6 @@
             )
         return jnp.concatenate(grads, axis=1), windows(z, p)
 
-    line = range(1, nz)
-    flat = range(1, plane)
 
     for z in up:
         plane_arrive(2, grad2, needs(up, z))
@@ -457,12 +466,12 @@
     folded = (folded[0:32] + folded[32:64]).astype(BF16)
     qs[0], qs[1] = folded[0:16], folded[16:32]
     qrc[slot] = qs[core]
-    for off in range(plane):
+    for off in whole_plane:
         if off > 0:
             to_plane(1, off, qs.at[core], qrc.at[slot]).start()
         to_plane(1, off, qs.at[other], qrc.at[slot], True).start()
 
-    for off in range(plane):
+    for off in whole_plane:
         if off > 0:
             scatter(off).wait_recv()
         scatter(off, True).wait_recv()
@@ -478,7 +487,7 @@
     for copy in out_copies(1, half2, grads_out):
         copy.start()
 
-    for off in range(plane):
+    for off in whole_plane:
         if off > 0:
             to_plane(1, off, qs.at[core], qrc.at[slot]).wait_recv()
         to_plane(1, off, qs.at[other], qrc.at[slot], True).wait_recv()
@@ -488,7 +497,7 @@
     total = total.astype(BF16)
     qsc[...] = total
     qrb[core, iz] = total
-    for off in range(nz):
+    for off in whole_line:
         if off > 0:
             to_line(1, off, qsc, qrb.at[core, iz]).start()
         to_line(1, off, qsc, qrb.at[core, iz], True).start()
@@ -499,12 +508,12 @@
     for q in range(1, nz):
         total = total + rc[q].astype(F32)
     fd[core, me_plane] = (total * (1.0 / batch)).astype(BF16)
-    for off in range(plane):
+    for off in whole_plane:
         if off > 0:
             to_plane(2, off, fd.at[core, me_plane], fd.at[core, me_plane]).start()
         to_plane(2, off, fd.at[core, me_plane], fd.at[core, me_plane], True).start()
 
-    for off in range(nz):
+    for off in whole_line:
         if off > 0:
             to_line(1, off, qsc, qrb.at[core, iz]).wait_recv()
         to_line(1, off, qsc, qrb.at[core, iz], True).wait_recv()
@@ -517,7 +526,7 @@
     turned = jnp.transpose(jnp.concatenate(halves, axis=0))
     for d in range(27):
         one_out[d] = turned[4 * d : 4 * d + 4, :]
-    for off in range(plane):
+    for off in whole_plane:
         if off > 0:
             to_plane(2, off, fd.at[core, me_plane], fd.at[core, me_plane]).wait_recv()
         to_plane(2, off, fd.at[core, me_plane], fd.at[core, me_plane], True).wait_recv()
@@ -541,9 +550,9 @@
         scatter(off).wait_send()
         to_plane(1, off, qs.at[core], qrc.at[slot]).wait_send()
         to_plane(2, off, fd.at[core, me_plane], fd.at[core, me_plane]).wait_send()
-    for off in range(nz):
+    for off in whole_line:
         to_line(1, off, qsc, qrb.at[core, iz], True).wait_send()
-    for off in range(plane):
+    for off in whole_plane:
         scatter(off, True).wait_send()
         to_plane(1, off, qs.at[other], qrc.at[slot], True).wait_send()
         to_plane(2, off, fd.at[core, me_plane], fd.at[core, me_plane], True).wait_send()

time: 41.7 us -> 40.8 us (0.978)
  Pallas kernels: 41 us -> 40.1 us
    pallas_call x1, Pallas kernels: 40 us -> 39.1 us  [per_device(): pl.pallas_call(functools.partial(step_kernel, dims), out_shape=tuple((vme...]
where the time goes in v5:
time: 40.8 us; the launch traced here: 40.7 us
  Pallas kernels  40.1 us (98%)
  between operations  0.64 us (2%)
    pallas_call x1, Pallas kernels, per_device(): pl.pallas_call(functools.partial(step_kernel, dims), out_shape=tuple((vme...  39.1 us
    pallas_call x1, Pallas kernels, per_device(): pl.pallas_call(leave_kernel, out_shape=tuple((jax.ShapeDtypeStruct(shape,...  0.99 us

profile of v5, /device:TPU:1, one launch (start us, length us, event | category | flops | bytes accessed | tf_op | source)
XLA Modules:
  0.0 40.7 jit_solution(4185773640121227164)
XLA Ops:
  0.6 39.1 %shard_map.75 = (bf16[2,512,128]{2,1,0:T(8,128)(2,1)S(1)}, bf16[2,512,128]{2,1,0:T(8,128)(2,1)S(1)}, f32[27,4,32]{2,1,0:T(4,128)S(1)}, f32[27,32,64]{2,1,0:T(8,128)S(1)}) custom-call(bf16[2,512,128]{2,1,0:T(8,128)(2,1)} %bitcast.16, bf16[27,4,32]{2,1,0:T(4,128)(2,1)} %bitcast.19, bf16[27,32,64]{2,1,0:T(8,128)(2,1)} %bitcast.17, bf16[2,64,4,64]{3,2,1,0:T(4,128)(2,1)} %bitcast.18), custom_call_target="tpu_custom_call" | custom-call | tf_op jit(solution)/shard_map/pallas_call | solution.py:591
  39.7 1.0 %shard_map.76 = (bf16[2,512,128]{2,1,0:T(8,128)(2,1)}, bf16[2,512,128]{2,1,0:T(8,128)(2,1)}, f32[27,4,32]{2,1,0:T(4,128)}, f32[27,32,64]{2,1,0:T(8,128)}) custom-call(bf16[2,512,128]{2,1,0:T(8,128)(2,1)S(1)} %get-tuple-element.12.refs_0_, bf16[2,512,128]{2,1,0:T(8,128)(2,1)S(1)} %get-tuple-element.13.refs_1_, f32[27,4,32]{2,1,0:T(4,128)S(1)} %get-tuple-element.14.refs_2_, ...), custom_call_target="tpu_custom_call" | custom-call | tf_op jit(solution)/shard_map/pallas_call | solution.py:639

commit v6 on v5

--- a/solution.py
+++ b/solution.py
@@ -114,15 +114,17 @@
         )
 
     turns = tuple(
-        (p, dz, dy)
+        (p, dz, dy, h)
         for p in range(sz)
         for dz, dy in DIRS
         if dz == 0 or p == (0 if dz == -1 else sz - 1)
+        for h in range(2)
+        if dy == 0 or h == (0 if dy == -1 else 1)
     )
 
     def plane_copy(k, ref, m):
-        p, dz, dy = turns[m]
-        fy, ty = part(dy, ref.shape[1] - 2)
+        p, dz, dy, h = turns[m]
+        fy, ty = part(dy, sy) if dy else (pl.ds(1 + h * (sy // 2), sy // 2),) * 2
         to_z = p + 1 if dz == 0 else (0 if dz == 1 else sz + 1)
         return pltpu.make_async_remote_copy(
             src_ref=ref.at[p + 1, fy],
@@ -133,28 +135,34 @@
             device_id_type=MESH,
         )
 
-    def plane_send(k, ref, p):
-        for m, (q, dz, dy) in enumerate(turns):
-            if q == p:
-
-                @pl.when(exists(dz, dy))
+    def plane_send(k, ref, p, half):
+        for d in DIRS:
+            group = [m for m, (q, dz, dy, h) in enumerate(turns) if q == p and (dz, dy) == d and h == half]
+            if group:
+
+                @pl.when(exists(*d))
                 def _():
-                    plane_copy(k, ref, m).start()
+                    for m in group:
+                        plane_copy(k, ref, m).start()
 
     def plane_arrive(k, ref, wanted):
-        for m, (q, dz, dy) in enumerate(turns):
-            if dz in wanted:
-
-                @pl.when(exists(-dz, -dy))
+        for d in DIRS:
+            group = [m for m, (q, dz, dy, h) in enumerate(turns) if (dz, dy) == d and dz in wanted]
+            if group:
+
+                @pl.when(exists(-d[0], -d[1]))
                 def _():
-                    plane_copy(k, ref, m).wait_recv()
+                    for m in group:
+                        plane_copy(k, ref, m).wait_recv()
 
     def planes_sent(k, ref):
-        for m, (q, dz, dy) in enumerate(turns):
-
-            @pl.when(exists(dz, dy))
+        for d in DIRS:
+            group = [m for m, (q, dz, dy, h) in enumerate(turns) if (dz, dy) == d]
+
+            @pl.when(exists(*d))
             def _():
-                plane_copy(k, ref, m).wait_send()
+                for m in group:
+                    plane_copy(k, ref, m).wait_send()
 
     def halo_clear(ref):
         for dz, dy in DIRS:
@@ -353,8 +361,9 @@
     hear_word(1)
     spread_word(2)
     for z in up:
-        loop_pairs(z, first_pair)
-        plane_send(1, pool, z)
+        for h in range(2):
+            loop_pairs(z, first_pair, h * (sy // 4), (h + 1) * (sy // 4))
+            plane_send(1, pool, z, h)
     hear_word(2)
     spread_word(3)
     half1[...] = flat1[...].astype(BF16)
@@ -396,8 +405,9 @@
 
     for z in down:
         plane_arrive(1, pool, needs(down, z))
-        loop_pairs(z, second_pair)
-        plane_send(2, grad2, z)
+        for h in range(2):
+            loop_pairs(z, second_pair, h * (sy // 4), (h + 1) * (sy // 4))
+            plane_send(2, grad2, z, h)
 
     hear_word(3)
 
@@ -627,7 +637,7 @@
                 vmem((16, 128), BF16),
                 vmem((2 * plane, 16, 128), BF16),
                 dma((6,)), dma((2,)), dma((2,)),
-                dma((3, 6 + 2 * sz)), dma((3, 6 + 2 * sz)),
+                dma((3, 8 + 2 * sz)), dma((3, 8 + 2 * sz)),
                 pltpu.SemaphoreType.REGULAR((4,)),
                 dma((2, 2 * nz - 1)), dma((2, 2 * nz - 1)),
                 dma((3, 2 * plane - 1)), dma((3, 2 * plane - 1)),

time: 40.8 us -> 40.7 us (level)
  no operation moved by 1% of the time
where the time goes in v6:
time: 40.7 us; the launch traced here: 40.6 us
  Pallas kernels  39.9 us (98%)
  between operations  0.64 us (2%)
    pallas_call x1, Pallas kernels, per_device(): pl.pallas_call(functools.partial(step_kernel, dims), out_shape=tuple((vme...  38.9 us
    pallas_call x1, Pallas kernels, per_device(): pl.pallas_call(leave_kernel, out_shape=tuple((jax.ShapeDtypeStruct(shape,...  0.99 us

profile of v6, /device:TPU:1, one launch (start us, length us, event | category | flops | bytes accessed | tf_op | source)
XLA Modules:
  0.0 40.6 jit_solution(14792880245045690741)
XLA Ops:
  0.6 38.9 %shard_map.75 = (bf16[2,512,128]{2,1,0:T(8,128)(2,1)S(1)}, bf16[2,512,128]{2,1,0:T(8,128)(2,1)S(1)}, f32[27,4,32]{2,1,0:T(4,128)S(1)}, f32[27,32,64]{2,1,0:T(8,128)S(1)}) custom-call(bf16[2,512,128]{2,1,0:T(8,128)(2,1)} %bitcast.16, bf16[27,4,32]{2,1,0:T(4,128)(2,1)} %bitcast.19, bf16[27,32,64]{2,1,0:T(8,128)(2,1)} %bitcast.17, bf16[2,64,4,64]{3,2,1,0:T(4,128)(2,1)} %bitcast.18), custom_call_target="tpu_custom_call" | custom-call | tf_op jit(solution)/shard_map/pallas_call | solution.py:601
  39.6 1.0 %shard_map.76 = (bf16[2,512,128]{2,1,0:T(8,128)(2,1)}, bf16[2,512,128]{2,1,0:T(8,128)(2,1)}, f32[27,4,32]{2,1,0:T(4,128)}, f32[27,32,64]{2,1,0:T(8,128)}) custom-call(bf16[2,512,128]{2,1,0:T(8,128)(2,1)S(1)} %get-tuple-element.12.refs_0_, bf16[2,512,128]{2,1,0:T(8,128)(2,1)S(1)} %get-tuple-element.13.refs_1_, f32[27,4,32]{2,1,0:T(4,128)S(1)} %get-tuple-element.14.refs_2_, ...), custom_call_target="tpu_custom_call" | custom-call | tf_op jit(solution)/shard_map/pallas_call | solution.py:649
